TPU v7x, 32 devices: a whole 2x2x4 slice. The times are simulated.
32 devices in a mesh: ctx: 8 (over y, x, core), fsdp: 4 (over z).
Axes of the slice: x: 2, y: 2, z: 4, core: 2. Of those that a mesh axis runs over, the one named last changes fastest.
Arguments:
- layer_in: bfloat16 [8, 1024, 1024], P('fsdp', 'ctx'), may hold values from -6 to 6
- block_order: int32 [8, 16], P('fsdp'), may hold values from 0 to 15, as said below
- ln1_gain: bfloat16 [1024], P('fsdp'), may hold values from 0.5 to 1.5
- ln1_shift: bfloat16 [1024], P('fsdp'), may hold values from -3 to 3
- w_qkv: bfloat16 [1024, 3072], P('fsdp'), may hold values from -0.1875 to 0.1875
- b_query: bfloat16 [1024], P('fsdp'), may hold values from -3 to 3
- b_value: bfloat16 [1024], P('fsdp'), may hold values from -3 to 3
- w_out: bfloat16 [1024, 1024], P('fsdp'), may hold values from -1 to 1
- b_out: bfloat16 [1024], P('fsdp'), may hold values from -2 to 2
- ln2_gain: bfloat16 [1024], P('fsdp'), may hold values from 0.5 to 1.5
- ln2_shift: bfloat16 [1024], P('fsdp'), may hold values from -3 to 3
- w_up: bfloat16 [1024, 4096], P('fsdp'), may hold values from -0.1875 to 0.1875
- b_up: bfloat16 [4096], P('fsdp'), may hold values from -3 to 3
- w_down: bfloat16 [4096, 1024], P('fsdp'), may hold values from -0.09375 to 0.09375
- b_down: bfloat16 [1024], P('fsdp'), may hold values from -3 to 3
- cotangent: bfloat16 [8, 1024, 1024], P('fsdp', 'ctx'), may hold values from -6 to 6
Outputs:
- layer_out: bfloat16 [8, 1024, 1024], P('fsdp', 'ctx')
- input_grad: bfloat16 [8, 1024, 1024], P('fsdp', 'ctx')
- grad_ln1_gain: float32 [1024], P(('ctx', 'fsdp'))
- grad_ln1_shift: float32 [1024], P(('ctx', 'fsdp'))
- grad_w_qkv: float32 [1024, 3072], P(('ctx', 'fsdp'))
- grad_b_query: float32 [1024], P(('ctx', 'fsdp'))
- grad_b_value: float32 [1024], P(('ctx', 'fsdp'))
- grad_w_out: float32 [1024, 1024], P(('ctx', 'fsdp'))
- grad_b_out: float32 [1024], P(('ctx', 'fsdp'))
- grad_ln2_gain: float32 [1024], P(('ctx', 'fsdp'))
- grad_ln2_shift: float32 [1024], P(('ctx', 'fsdp'))
- grad_w_up: float32 [1024, 4096], P(('ctx', 'fsdp'))
- grad_b_up: float32 [4096], P(('ctx', 'fsdp'))
- grad_w_down: float32 [4096, 1024], P(('ctx', 'fsdp'))
- grad_b_down: float32 [1024], P(('ctx', 'fsdp'))
Inputs may be any that keep to these rules, and one draw needn't show every extreme that they name: Stored block j of sequence s (rows j * 64 to (j + 1) * 64 - 1 as stored) holds block block_order[s, j] of the true order; each row is a permutation, and entry 2c + 1 is 15 minus entry 2c.
All inputs are finite; a program needn't handle non-finite values.
Results may differ from a plain program's by a relative error of at most 0.012.
Values may be sent and summed in bfloat16 or wider, within the bound.
A program may use at most 512 MiB of HBM per device.

v0:
```python
import math

import jax
import jax.numpy as jnp
from jax import lax
from jax.sharding import PartitionSpec as P

D = 1024
HEADS = 8
HEAD_DIM = 128


EPSILON = 1e-05
NEG_LARGE = -1e30
GELU_C = math.sqrt(2.0 / math.pi)
GELU_K = 0.044715


def gelu_tanh(values):
    inner = jnp.tanh(GELU_C * (values + GELU_K * values * values * values))
    return 0.5 * values * (1.0 + inner)


def gelu_slope(values):
    inner = jnp.tanh(GELU_C * (values + GELU_K * values * values * values))
    return 0.5 * (1.0 + inner) + 0.5 * values * (1.0 - inner * inner) * GELU_C * (
        1.0 + 3.0 * GELU_K * values * values
    )


def normalize(values, gain_vec, shift_vec):
    average = jnp.mean(values, axis=-1, keepdims=True)
    centered = values - average
    inv_dev = lax.rsqrt(jnp.mean(centered * centered, axis=-1, keepdims=True) + EPSILON)
    normed = centered * inv_dev
    return (normed * gain_vec + shift_vec, normed, inv_dev)


def normalize_back(grad, normed, inv_dev, gain_vec):
    scaled = grad * gain_vec
    return inv_dev * (
        scaled
        - jnp.mean(scaled, axis=-1, keepdims=True)
        - normed * jnp.mean(scaled * normed, axis=-1, keepdims=True)
    )


def token_positions(order_row, seq_len, half_rows):
    rows = jnp.arange(seq_len, dtype=jnp.int32)
    slots = jnp.arange(order_row.shape[0], dtype=jnp.int32)
    picked = jnp.sum(
        jnp.where((rows // half_rows)[:, None] == slots[None, :], order_row[None, :], 0), axis=1
    )
    return picked * half_rows + rows % half_rows


def block_probs(query_heads, key_heads, query_pos, key_pos, row_lse, scale):
    raw_scores = jnp.einsum(
        "qhd,khd->hqk", query_heads, key_heads, preferred_element_type=jnp.float32
    )
    allowed = (query_pos[:, None] >= key_pos[None, :])[None]
    shifted = jnp.where(allowed, raw_scores * scale - row_lse[:, :, None], NEG_LARGE)
    return jnp.where(allowed, jnp.exp(shifted), 0.0)


def score_grads(probs, grad_probs, row_delta, scale):
    return (probs * (grad_probs - row_delta[:, :, None]) * scale).astype(jnp.bfloat16)


def per_device(
    layer_in,
    block_order,
    ln1_gain,
    ln1_shift,
    w_qkv,
    b_query,
    b_value,
    w_out,
    b_out,
    ln2_gain,
    ln2_shift,
    w_up,
    b_up,
    w_down,
    b_down,
    cotangent,
):
    full = (
        lax.all_gather(ln1_gain, "fsdp", axis=0, tiled=True),
        lax.all_gather(ln1_shift, "fsdp", axis=0, tiled=True),
        lax.all_gather(w_qkv, "fsdp", axis=0, tiled=True),
        lax.all_gather(b_query, "fsdp", axis=0, tiled=True),
        lax.all_gather(b_value, "fsdp", axis=0, tiled=True),
        lax.all_gather(w_out, "fsdp", axis=0, tiled=True),
        lax.all_gather(b_out, "fsdp", axis=0, tiled=True),
        lax.all_gather(ln2_gain, "fsdp", axis=0, tiled=True),
        lax.all_gather(ln2_shift, "fsdp", axis=0, tiled=True),
        lax.all_gather(w_up, "fsdp", axis=0, tiled=True),
        lax.all_gather(b_up, "fsdp", axis=0, tiled=True),
        lax.all_gather(w_down, "fsdp", axis=0, tiled=True),
        lax.all_gather(b_down, "fsdp", axis=0, tiled=True),
    )
    qkv_full, out_full, up_full, down_full = (full[2], full[5], full[9], full[11])
    first_gain = full[0].astype(jnp.float32)
    first_shift = full[1].astype(jnp.float32)
    query_bias = full[3].astype(jnp.float32)
    value_bias = full[4].astype(jnp.float32)
    out_bias = full[6].astype(jnp.float32)
    second_gain = full[7].astype(jnp.float32)
    second_shift = full[8].astype(jnp.float32)
    up_bias = full[10].astype(jnp.float32)
    down_bias = full[12].astype(jnp.float32)
    micro = layer_in.shape[0]
    tokens = layer_in.shape[1]
    seq_len = tokens * lax.axis_size("ctx")
    half_rows = tokens // 2
    key_block = min(512, seq_len)
    blocks = seq_len // key_block
    scale = HEAD_DIM ** (-0.5)
    here = lax.axis_index("ctx")
    heads_shape = (blocks, key_block, HEADS, HEAD_DIM)
    totals = [jnp.zeros(item.shape, jnp.float32) for item in full]
    outputs_fwd = []
    outputs_grad = []
    for micro_step in range(micro):
        pos_all = token_positions(block_order[micro_step], seq_len, half_rows)
        pos_mine = lax.dynamic_slice_in_dim(pos_all, here * tokens, tokens)
        pos_blocks = pos_all.reshape(blocks, key_block)
        inputs = layer_in[micro_step].astype(jnp.float32)
        first_out, first_normed, first_inv = normalize(inputs, first_gain, first_shift)
        first_low = first_out.astype(jnp.bfloat16)
        projected = jnp.dot(first_low, qkv_full, preferred_element_type=jnp.float32)
        query_low = (projected[:, :D] + query_bias).astype(jnp.bfloat16)
        key_low = projected[:, D : 2 * D].astype(jnp.bfloat16)
        value_low = (projected[:, 2 * D :] + value_bias).astype(jnp.bfloat16)
        keys_all, values_all = (
            lax.all_gather(key_low, "ctx", axis=0, tiled=True),
            lax.all_gather(value_low, "ctx", axis=0, tiled=True),
        )
        query_heads = query_low.reshape(tokens, HEADS, HEAD_DIM)
        key_blocks = keys_all.reshape(heads_shape)
        value_blocks = values_all.reshape(heads_shape)

        def stats_step(carry, piece):
            run_max, run_sum = carry
            key_piece, key_pos = piece
            raw_scores = (
                jnp.einsum(
                    "qhd,khd->hqk", query_heads, key_piece, preferred_element_type=jnp.float32
                )
                * scale
            )
            allowed = (pos_mine[:, None] >= key_pos[None, :])[None]
            masked = jnp.where(allowed, raw_scores, NEG_LARGE)
            new_max = jnp.maximum(run_max, jnp.max(masked, axis=-1))
            weights = jnp.where(allowed, jnp.exp(masked - new_max[:, :, None]), 0.0)
            run_sum = run_sum * jnp.exp(run_max - new_max) + jnp.sum(weights, axis=-1)
            return ((new_max, run_sum), None)

        start_state = (
            jnp.full((HEADS, tokens), NEG_LARGE, jnp.float32),
            jnp.zeros((HEADS, tokens), jnp.float32),
        )
        (run_max, run_sum), unused = lax.scan(stats_step, start_state, (key_blocks, pos_blocks))
        row_lse = run_max + jnp.log(run_sum)

        def output_step(carry, piece):
            acc_low, acc_exact = carry
            key_piece, value_piece, key_pos = piece
            probs = block_probs(query_heads, key_piece, pos_mine, key_pos, row_lse, scale)
            acc_low = acc_low + jnp.einsum(
                "hqk,khd->hqd",
                probs.astype(jnp.bfloat16),
                value_piece,
                preferred_element_type=jnp.float32,
            )
            acc_exact = acc_exact + jnp.einsum(
                "hqk,khd->hqd",
                probs,
                value_piece.astype(jnp.float32),
                preferred_element_type=jnp.float32,
            )
            return ((acc_low, acc_exact), None)

        start_acc = (
            jnp.zeros((HEADS, tokens, HEAD_DIM), jnp.float32),
            jnp.zeros((HEADS, tokens, HEAD_DIM), jnp.float32),
        )
        (attn_heads, exact_heads), unused = lax.scan(
            output_step, start_acc, (key_blocks, value_blocks, pos_blocks)
        )
        attn_low = jnp.transpose(attn_heads, (1, 0, 2)).reshape(tokens, D).astype(jnp.bfloat16)
        resid = inputs + jnp.dot(attn_low, out_full, preferred_element_type=jnp.float32) + out_bias
        second_out, second_normed, second_inv = normalize(resid, second_gain, second_shift)
        second_low = second_out.astype(jnp.bfloat16)
        hidden = jnp.dot(second_low, up_full, preferred_element_type=jnp.float32) + up_bias
        active_low = gelu_tanh(hidden).astype(jnp.bfloat16)
        result = (
            resid + jnp.dot(active_low, down_full, preferred_element_type=jnp.float32) + down_bias
        )
        outputs_fwd.append(result.astype(jnp.bfloat16))
        grad_out = cotangent[micro_step]
        grad_outf = grad_out.astype(jnp.float32)
        term_down = jnp.einsum(
            "tf,td->fd", active_low, grad_out, preferred_element_type=jnp.float32
        )
        grad_active = jnp.einsum(
            "td,fd->tf", grad_out, down_full, preferred_element_type=jnp.float32
        )
        grad_hidden = (grad_active * gelu_slope(hidden)).astype(jnp.bfloat16)
        term_up = jnp.einsum(
            "td,tf->df", second_low, grad_hidden, preferred_element_type=jnp.float32
        )
        grad_second = jnp.einsum(
            "tf,df->td", grad_hidden, up_full, preferred_element_type=jnp.float32
        )
        grad_resid = grad_outf + normalize_back(grad_second, second_normed, second_inv, second_gain)
        grad_branch = grad_resid.astype(jnp.bfloat16)
        term_out = jnp.einsum(
            "td,te->de", attn_low, grad_branch, preferred_element_type=jnp.float32
        )
        grad_attn = jnp.einsum(
            "te,de->td", grad_branch, out_full, preferred_element_type=jnp.float32
        ).astype(jnp.bfloat16)
        grad_heads = grad_attn.reshape(tokens, HEADS, HEAD_DIM)
        row_delta = jnp.einsum("qhd,hqd->hq", grad_heads.astype(jnp.float32), exact_heads)

        def backward_step(grad_query, piece):
            key_piece, value_piece, key_pos = piece
            probs = block_probs(query_heads, key_piece, pos_mine, key_pos, row_lse, scale)
            grad_value = jnp.einsum(
                "hqk,qhd->khd",
                probs.astype(jnp.bfloat16),
                grad_heads,
                preferred_element_type=jnp.float32,
            )
            grad_probs = jnp.einsum(
                "qhd,khd->hqk", grad_heads, value_piece, preferred_element_type=jnp.float32
            )
            grad_scores = score_grads(probs, grad_probs, row_delta, scale)
            grad_query = grad_query + jnp.einsum(
                "hqk,khd->qhd", grad_scores, key_piece, preferred_element_type=jnp.float32
            )
            grad_key = jnp.einsum(
                "hqk,qhd->khd", grad_scores, query_heads, preferred_element_type=jnp.float32
            )
            rows_here = key_piece.shape[0]
            return (
                grad_query,
                jnp.concatenate(
                    [grad_key.reshape(rows_here, D), grad_value.reshape(rows_here, D)], axis=1
                ),
            )

        grad_query, key_terms = lax.scan(
            backward_step,
            jnp.zeros((tokens, HEADS, HEAD_DIM), jnp.float32),
            (key_blocks, value_blocks, pos_blocks),
        )
        key_sums = lax.psum_scatter(
            key_terms.reshape(seq_len, 2 * D), "ctx", scatter_dimension=0, tiled=True
        )
        grad_key_low = key_sums[:, :D].astype(jnp.bfloat16)
        grad_value_low = key_sums[:, D:].astype(jnp.bfloat16)
        grad_query_low = grad_query.reshape(tokens, D).astype(jnp.bfloat16)
        grad_projected = jnp.concatenate([grad_query_low, grad_key_low, grad_value_low], axis=1)
        term_qkv = jnp.einsum(
            "td,te->de", first_low, grad_projected, preferred_element_type=jnp.float32
        )
        grad_first = jnp.einsum(
            "te,de->td", grad_projected, qkv_full, preferred_element_type=jnp.float32
        )
        grad_input = grad_resid + normalize_back(grad_first, first_normed, first_inv, first_gain)
        outputs_grad.append(grad_input.astype(jnp.bfloat16))
        terms = (
            jnp.sum(grad_first * first_normed, axis=0),
            jnp.sum(grad_first, axis=0),
            term_qkv,
            jnp.sum(grad_query_low.astype(jnp.float32), axis=0),
            jnp.sum(grad_value_low.astype(jnp.float32), axis=0),
            term_out,
            jnp.sum(grad_branch.astype(jnp.float32), axis=0),
            jnp.sum(grad_second * second_normed, axis=0),
            jnp.sum(grad_second, axis=0),
            term_up,
            jnp.sum(grad_hidden.astype(jnp.float32), axis=0),
            term_down,
            jnp.sum(grad_outf, axis=0),
        )
        totals = [older + newer for older, newer in zip(totals, terms)]
    summed = (
        lax.psum_scatter(totals[0], ("ctx", "fsdp"), scatter_dimension=0, tiled=True),
        lax.psum_scatter(totals[1], ("ctx", "fsdp"), scatter_dimension=0, tiled=True),
        lax.psum_scatter(totals[2], ("ctx", "fsdp"), scatter_dimension=0, tiled=True),
        lax.psum_scatter(totals[3], ("ctx", "fsdp"), scatter_dimension=0, tiled=True),
        lax.psum_scatter(totals[4], ("ctx", "fsdp"), scatter_dimension=0, tiled=True),
        lax.psum_scatter(totals[5], ("ctx", "fsdp"), scatter_dimension=0, tiled=True),
        lax.psum_scatter(totals[6], ("ctx", "fsdp"), scatter_dimension=0, tiled=True),
        lax.psum_scatter(totals[7], ("ctx", "fsdp"), scatter_dimension=0, tiled=True),
        lax.psum_scatter(totals[8], ("ctx", "fsdp"), scatter_dimension=0, tiled=True),
        lax.psum_scatter(totals[9], ("ctx", "fsdp"), scatter_dimension=0, tiled=True),
        lax.psum_scatter(totals[10], ("ctx", "fsdp"), scatter_dimension=0, tiled=True),
        lax.psum_scatter(totals[11], ("ctx", "fsdp"), scatter_dimension=0, tiled=True),
        lax.psum_scatter(totals[12], ("ctx", "fsdp"), scatter_dimension=0, tiled=True),
    )
    return (
        jnp.stack(outputs_fwd),
        jnp.stack(outputs_grad),
        summed[0],
        summed[1],
        summed[2],
        summed[3],
        summed[4],
        summed[5],
        summed[6],
        summed[7],
        summed[8],
        summed[9],
        summed[10],
        summed[11],
        summed[12],
    )


def solution(mesh):
    placed = (
        P("fsdp", "ctx", None),
        P("fsdp", None),
        P("fsdp"),
        P("fsdp"),
        P("fsdp", None),
        P("fsdp"),
        P("fsdp"),
        P("fsdp", None),
        P("fsdp"),
        P("fsdp"),
        P("fsdp"),
        P("fsdp", None),
        P("fsdp"),
        P("fsdp", None),
        P("fsdp"),
        P("fsdp", "ctx", None),
    )
    return jax.shard_map(
        per_device,
        mesh=mesh,
        in_specs=placed,
        out_specs=(
            P("fsdp", "ctx", None),
            P("fsdp", "ctx", None),
            P(("ctx", "fsdp")),
            P(("ctx", "fsdp")),
            P(("ctx", "fsdp"), None),
            P(("ctx", "fsdp")),
            P(("ctx", "fsdp")),
            P(("ctx", "fsdp"), None),
            P(("ctx", "fsdp")),
            P(("ctx", "fsdp")),
            P(("ctx", "fsdp")),
            P(("ctx", "fsdp"), None),
            P(("ctx", "fsdp")),
            P(("ctx", "fsdp"), None),
            P(("ctx", "fsdp")),
        ),
        check_vma=False,
    )
```

profile of v0, /device:TPU:0, one launch (start us, length us, event | category | flops | bytes accessed | tf_op | source)
XLA Modules:
  0.0 1857.9 jit_solution(17294477554371182860)
XLA Ops:
  9.3 12.6 all-gather.1
  21.9 7.8 all-gather
  31.3 96.4 %all-gather.17.cloned.1.call-done = bf16[1024,3072]{1,0:T(8,128)(2,1)} async-done(((bf16[256,3072]{1,0:T(8,128)(2,1)}), bf16[1024,3072]{1,0:T(8,128)(2,1)}) %all-gather.17.cloned.1.call-update) | async-done | bytes 6291472 | tf_op jit(solution)/shard_map/all_gather | solution.py:91
  127.7 3.9 fusion.169
  132.4 7.9 all-gather.3
  140.4 9.2 all-gather.2
  159.8 8.3 all-gather.6
  168.1 8.9 all-gather.5
  176.9 8.3 all-gather.4
  185.2 12.0 all_gather.63
  207.3 11.5 all-gather.21.cloned.1.call-done
  221.4 27.1 %all-gather.19.cloned.1.call-done = bf16[1024,1024]{1,0:T(8,128)(2,1)} async-done(((bf16[128,1024]{1,0:T(8,128)(2,1)}), bf16[1024,1024]{1,0:T(8,128)(2,1)}) %all-gather.19.cloned.1.call-update) | async-done | bytes 2097168 | tf_op jit(solution)/shard_map/all_gather | solution.py:137
  252.4 5.0 while.80
  257.4 10.1 while.81
  269.4 4.9 while.78
  274.2 7.6 while.79
  282.7 13.1 all-gather.23.cloned.1.call-done
  299.8 146.0 %all-gather.25.cloned.1.call-done = bf16[1024,4096]{1,0:T(8,128)(2,1)} async-done(((bf16[256,4096]{1,0:T(8,128)(2,1)}), bf16[1024,4096]{1,0:T(8,128)(2,1)}) %all-gather.25.cloned.1.call-update) | async-done | bytes 8388624 | tf_op jit(solution)/shard_map/all_gather | solution.py:98
  445.8 6.1 convolution_add_fusion.7
  451.9 143.4 %all-gather.27.cloned.1.call-done = bf16[4096,1024]{1,0:T(8,128)(2,1)} async-done(((bf16[1024,1024]{1,0:T(8,128)(2,1)}), bf16[4096,1024]{1,0:T(8,128)(2,1)}) %all-gather.27.cloned.1.call-update) | async-done | bytes 8388624 | tf_op jit(solution)/shard_map/all_gather | solution.py:100
  595.2 8.3 convert_reduce_fusion
  609.7 4.3 convert_reduce_fusion.1
  622.9 4.3 broadcast.392.clone2
  627.2 35.6 %while.83 = (s32[]{:T(128)}, f32[128,8,128]{0,2,1:T(8,128)S(1)}, f32[2,512,2048]{2,1,0:T(8,128)}, bf16[2,512,8,128]{3,1,2,0:T(8,128)(2,1)}, s32[128]{0:T(128)S(1...) while((s32[]{:T(128)}, f32[128,8,128]{0,2,1:T(8,128)S(1)}, ...), condition=%wide.region_32.33_spmd.clone, body=%wide.region_31.32_spmd.clone.sunk | while | flops 677183488 | bytes 60963544 | solution.py:255
  634.9 5.4 copy.272
  640.3 4.6 constant_dynamic-update-slice_fusion.5
  652.6 5.4 copy.272
  658.1 4.7 constant_dynamic-update-slice_fusion.5
  673.3 4.7 broadcast.392.clone2.1
  678.0 36.3 %while.82 = (s32[]{:T(128)}, f32[128,8,128]{0,2,1:T(8,128)S(1)}, f32[2,512,2048]{2,1,0:T(8,128)}, bf16[2,512,8,128]{3,1,2,0:T(8,128)(2,1)}, s32[128]{0:T(128)S(1...) while((s32[]{:T(128)}, f32[128,8,128]{0,2,1:T(8,128)S(1)}, ...), condition=%wide.region_25.26_spmd.clone, body=%wide.region_24.25_spmd.clone.sunk | while | flops 677183488 | bytes 53623516 | solution.py:255
  685.8 5.8 copy.271
  691.6 4.9 constant_dynamic-update-slice_fusion.4
  704.2 5.5 copy.271
  709.7 4.6 constant_dynamic-update-slice_fusion.4
  719.8 12.6 reduce-scatter.9.cloned.1.call-done
  733.7 73.7 %reduce-scatter.7.cloned.1.call-done = f32[128,2048]{1,0:T(8,128)} async-done(((f32[1024,2048]{1,0:T(8,128)}), f32[128,2048]{1,0:T(8,128)}) %reduce-scatter.7.cloned.1.call-update) | async-done | bytes 1048592 | tf_op jit(solution)/shard_map/reduce_scatter | solution.py:260
  811.6 6.4 convolution_add_fusion.6
  818.2 4.1 fusion.133
  822.4 9.1 convolution_add_fusion.4
  836.3 8.2 convolution_add_fusion.5
  845.2 11.1 all-gather.7
  856.5 5.7 fusion.88
  862.3 5.2 fusion.89
  873.3 38.9 %all-reduce.9 = (f32[1024]{0:T(1024)S(1)}, f32[1024]{0:T(1024)S(1)}, f32[1024]{0:T(1024)S(1)}, f32[1024]{0:T(1024)S(1)}, f32[1024]{0:T(1024)S(1)}, /*index=5*/f3...) all-reduce(f32[1024]{0:T(1024)S(1)} %add.391, ...), channel_id=4, replica_groups=mesh['ctx'=8,'fsdp'=4] {'ctx','fsdp'}, use_global_device_ids=true, to_apply=%region_38.39.clone | all-reduce | flops 12288 | bytes 98304
  918.8 40.4 %reduce-scatter.13.cloned.1.call-done = f32[32,1024]{1,0:T(8,128)} async-done(((f32[1024,1024]{1,0:T(8,128)}), f32[32,1024]{1,0:T(8,128)}) %reduce-scatter.13.cloned.1.call-update) | async-done | bytes 131088 | tf_op jit(solution)/shard_map/reduce_scatter | solution.py:297
  959.2 160.6 %reduce-scatter.11.cloned.1.call-done = f32[32,3072]{1,0:T(8,128)} async-done(((f32[1024,3072]{1,0:T(8,128)}), f32[32,3072]{1,0:T(8,128)}) %reduce-scatter.11.cloned.1.call-update) | async-done | bytes 393232 | tf_op jit(solution)/shard_map/reduce_scatter | solution.py:294
  1119.8 366.4 %reduce-scatter.17.cloned.1.call-done = f32[128,1024]{1,0:T(8,128)} async-done(((f32[4096,1024]{1,0:T(8,128)}), f32[128,1024]{1,0:T(8,128)}) %reduce-scatter.17.cloned.1.call-update) | async-done | bytes 524304 | tf_op jit(solution)/shard_map/reduce_scatter | solution.py:303
  1486.1 365.0 %reduce-scatter.15.cloned.1.call-done = f32[32,4096]{1,0:T(8,128)} async-done(((f32[1024,4096]{1,0:T(8,128)}), f32[32,4096]{1,0:T(8,128)}) %reduce-scatter.15.cloned.1.call-update) | async-done | bytes 524304 | tf_op jit(solution)/shard_map/reduce_scatter | solution.py:301
  (455 shorter events, 148.5 us)
Async XLA Ops:
  7.2 23.8 %copy-start.9 = (bf16[2,128,1024]{2,1,0:T(8,128)(2,1)S(1)}, bf16[2,128,1024]{2,1,0:T(8,128)(2,1)}, u32[]{:S(2)}) copy-start(bf16[2,128,1024]{2,1,0:T(8,128)(2,1)} %param.28) | copy-start | bytes 1572868
  7.2 120.5 %all-gather.17.cloned.1.call-start = ((), (), s32[]{:S(2)}) async-start(), calls=%async_computation.6 | async-start | bytes 7864320 | tf_op jit(solution)/shard_map/all_gather | solution.py:91
  7.9 191.5 %all-gather.29.cloned.1.call-start = ((), (), s32[]{:S(2)}) async-start(), calls=%async_computation.12 | async-start | bytes 2359296 | tf_op jit(solution)/shard_map/all_gather | solution.py:137
  21.9 127.7 %copy-start.50 = (f32[4,1,256]{2,1,0:T(1,128)}, f32[4,1,256]{2,1,0:T(1,128)S(1)}, u32[]{:S(2)}) copy-start(f32[4,1,256]{2,1,0:T(1,128)S(1)} %convert_element_type.245) | copy-start | bytes 12292
  29.7 119.9 %copy-start.48 = (f32[4,1,256]{2,1,0:T(1,128)}, f32[4,1,256]{2,1,0:T(1,128)S(1)}, u32[]{:S(2)}) copy-start(f32[4,1,256]{2,1,0:T(1,128)S(1)} %convert_element_type.244) | copy-start | bytes 12292
  30.9 100.6 %copy-start.57 = (f32[128]{0:T(128)}, f32[128]{0:T(128)S(1)}, u32[]{:S(2)}) copy-start(f32[128]{0:T(128)S(1)} %get-tuple-element.905) | copy-start | bytes 1540
  30.9 118.7 %copy-start.63 = (f32[128]{0:T(128)}, f32[128]{0:T(128)S(1)}, u32[]{:S(2)}) copy-start(f32[128]{0:T(128)S(1)} %get-tuple-element.906) | copy-start | bytes 1540
  31.2 100.3 %copy-start.79 = (f32[128]{0:T(128)}, f32[128]{0:T(128)S(1)}, u32[]{:S(2)}) copy-start(f32[128]{0:T(128)S(1)} %add_rsqrt_fusion.1) | copy-start | bytes 1540
  132.3 71.0 %all-gather.31.cloned.1.call-start = ((), (), s32[]{:S(2)}) async-start(), calls=%async_computation.13 | async-start | bytes 2359296 | tf_op jit(solution)/shard_map/all_gather | solution.py:138
  155.0 63.8 %all-gather.21.cloned.1.call-start = ((), (), s32[]{:S(2)}) async-start(), calls=%async_computation.8 | async-start | bytes 2359296 | tf_op jit(solution)/shard_map/all_gather | solution.py:138
  155.5 92.9 %all-gather.19.cloned.1.call-start = ((), (), s32[]{:S(2)}) async-start(), calls=%async_computation.7 | async-start | bytes 2359296 | tf_op jit(solution)/shard_map/all_gather | solution.py:137
  157.4 138.4 %all-gather.23.cloned.1.call-start = ((), (), s32[]{:S(2)}) async-start(), calls=%async_computation.9 | async-start | bytes 2621440 | tf_op jit(solution)/shard_map/all_gather | solution.py:94
  158.0 27.2 %copy-start.84 = (bf16[1024]{0:T(1024)(128)(2,1)S(1)}, bf16[1024]{0:T(1024)(128)(2,1)}, u32[]{:S(2)}) copy-start(bf16[1024]{0:T(1024)(128)(2,1)} %param.40) | copy-start | bytes 6148
  158.0 287.7 %all-gather.25.cloned.1.call-start = ((), (), s32[]{:S(2)}) async-start(), calls=%async_computation.10 | async-start | bytes 10485760 | tf_op jit(solution)/shard_map/all_gather | solution.py:98
  158.8 436.4 %all-gather.27.cloned.1.call-start = ((), (), s32[]{:S(2)}) async-start(), calls=%async_computation.11 | async-start | bytes 10485760 | tf_op jit(solution)/shard_map/all_gather | solution.py:100
  159.5 572.9 %reduce-scatter.9.cloned.1.call-start = ((), (), s32[]{:S(2)}) async-start(), calls=%async_computation.15 | async-start | bytes 9437184 | tf_op jit(solution)/shard_map/reduce_scatter | solution.py:260
  168.1 439.4 %copy-start.52 = (f32[4,1,256]{2,1,0:T(1,128)}, f32[4,1,256]{2,1,0:T(1,128)S(1)}, u32[]{:S(2)}) copy-start(f32[4,1,256]{2,1,0:T(1,128)S(1)} %convert_element_type.250) | copy-start | bytes 12292
  176.9 440.7 %copy-start.46 = (f32[4,1,256]{2,1,0:T(1,128)}, f32[4,1,256]{2,1,0:T(1,128)S(1)}, u32[]{:S(2)}) copy-start(f32[4,1,256]{2,1,0:T(1,128)S(1)} %convert_element_type.249) | copy-start | bytes 12292
  281.8 17.2 copy-start.42
  298.2 319.4 %copy-start.59 = (f32[128]{0:T(128)}, f32[128]{0:T(128)S(1)}, u32[]{:S(2)}) copy-start(f32[128]{0:T(128)S(1)} %broadcast_multiply_fusion.12) | copy-start | bytes 1540
  299.5 318.1 %copy-start.7 = (f32[128,1024]{1,0:T(8,128)}, f32[128,1024]{1,0:T(8,128)S(1)}, u32[]{:S(2)}) copy-start(f32[128,1024]{1,0:T(8,128)S(1)} %get-tuple-element.894) | copy-start | bytes 1572868
  299.6 318.1 %copy-start.61 = (f32[128]{0:T(128)}, f32[128]{0:T(128)S(1)}, u32[]{:S(2)}) copy-start(f32[128]{0:T(128)S(1)} %broadcast_multiply_fusion.10) | copy-start | bytes 1540
  299.8 317.9 %copy-start.67 = (f32[128]{0:T(128)}, f32[128]{0:T(128)S(1)}, u32[]{:S(2)}) copy-start(f32[128]{0:T(128)S(1)} %add_rsqrt_fusion.2) | copy-start | bytes 1540
  299.8 317.9 %copy-start.65 = (f32[128]{0:T(128)}, f32[128]{0:T(128)S(1)}, u32[]{:S(2)}) copy-start(f32[128]{0:T(128)S(1)} %add_rsqrt_fusion) | copy-start | bytes 1540
  445.8 149.5 %copy-start.45 = (bf16[2,128,1024]{2,1,0:T(8,128)(2,1)S(1)}, bf16[2,128,1024]{2,1,0:T(8,128)(2,1)}, u32[]{:S(2)}) copy-start(bf16[2,128,1024]{2,1,0:T(8,128)(2,1)} %param.43) | copy-start | bytes 1572868
  662.8 144.7 %reduce-scatter.7.cloned.1.call-start = ((), (), s32[]{:S(2)}) async-start(), calls=%async_computation.14 | async-start | bytes 9437184 | tf_op jit(solution)/shard_map/reduce_scatter | solution.py:260
  714.4 244.8 %reduce-scatter.13.cloned.1.call-start = ((), (), s32[]{:S(2)}) async-start(), calls=%async_computation.17 | async-start | bytes 4325376 | tf_op jit(solution)/shard_map/reduce_scatter | solution.py:297
  719.0 400.8 %reduce-scatter.11.cloned.1.call-start = ((), (), s32[]{:S(2)}) async-start(), calls=%async_computation.16 | async-start | bytes 12976128 | tf_op jit(solution)/shard_map/reduce_scatter | solution.py:294
  719.4 92.1 %copy-start.40 = (bf16[128,1024]{1,0:T(8,128)(2,1)}, bf16[128,1024]{1,0:T(8,128)(2,1)S(1)}, u32[]{:S(2)}) copy-start(bf16[128,1024]{1,0:T(8,128)(2,1)S(1)} %copy.214) | copy-start | bytes 786436
  719.4 90.2 %copy-start.10 = (bf16[2,128,1024]{2,1,0:T(8,128)(2,1)S(1)}, bf16[2,128,1024]{2,1,0:T(8,128)(2,1)}, u32[]{:S(2)}) copy-start(bf16[2,128,1024]{2,1,0:T(8,128)(2,1)} %param.28) | copy-start | bytes 1572868
  719.4 90.1 %copy-start.49 = (f32[4,1,256]{2,1,0:T(1,128)S(1)}, f32[4,1,256]{2,1,0:T(1,128)}, u32[]{:S(2)}) copy-start(f32[4,1,256]{2,1,0:T(1,128)} %copy-done.48) | copy-start | bytes 12292
  719.4 90.1 %copy-start.51 = (f32[4,1,256]{2,1,0:T(1,128)S(1)}, f32[4,1,256]{2,1,0:T(1,128)}, u32[]{:S(2)}) copy-start(f32[4,1,256]{2,1,0:T(1,128)} %copy-done.50) | copy-start | bytes 12292
  719.4 90.1 %copy-start.64 = (f32[128]{0:T(128)S(1)}, f32[128]{0:T(128)}, u32[]{:S(2)}) copy-start(f32[128]{0:T(128)} %copy-done.63) | copy-start | bytes 1540
  719.4 90.1 %copy-start.82 = (f32[128]{0:T(128)S(1)}, f32[128]{0:T(128)}, u32[]{:S(2)}) copy-start(f32[128]{0:T(128)} %copy-done.81) | copy-start | bytes 1540
  719.8 91.7 %copy-start.55 = (bf16[128,1024]{1,0:T(8,128)(2,1)}, bf16[128,1024]{1,0:T(8,128)(2,1)S(1)}, u32[]{:S(2)}) copy-start(bf16[128,1024]{1,0:T(8,128)(2,1)S(1)} %copy.213) | copy-start | bytes 786436
  733.7 77.8 %copy-start.32 = (bf16[128,2048]{1,0:T(8,128)(2,1)}, bf16[128,2048]{1,0:T(8,128)(2,1)S(1)}, u32[]{:S(2)}) copy-start(bf16[128,2048]{1,0:T(8,128)(2,1)S(1)} %convert.17) | copy-start | bytes 1572868
  818.0 668.2 %reduce-scatter.17.cloned.1.call-start = ((), (), s32[]{:S(2)}) async-start(), calls=%async_computation.19 | async-start | bytes 17301504 | tf_op jit(solution)/shard_map/reduce_scatter | solution.py:303
  831.6 1019.5 %reduce-scatter.15.cloned.1.call-start = ((), (), s32[]{:S(2)}) async-start(), calls=%async_computation.18 | async-start | bytes 17301504 | tf_op jit(solution)/shard_map/reduce_scatter | solution.py:301
  844.5 11.8 copy-start.72
  844.5 11.9 copy-start.69
  844.6 11.9 copy-start.70
  844.6 11.9 copy-start.75
  844.6 11.9 copy-start.76
  844.6 11.9 copy-start.73
  844.6 11.9 copy-start.74
  856.5 12.0 slice-start
  870.8 46.7 %copy-start.29 = (f32[128,1024]{1,0:T(8,128)S(1)}, f32[128,1024]{1,0:T(8,128)}, u32[]{:S(2)}) copy-start(f32[128,1024]{1,0:T(8,128)} %copy-done.27) | copy-start | bytes 1572868
  870.8 46.7 %copy-start.31 = (f32[128,1024]{1,0:T(8,128)S(1)}, f32[128,1024]{1,0:T(8,128)}, u32[]{:S(2)}) copy-start(f32[128,1024]{1,0:T(8,128)} %get-tuple-element.879) | copy-start | bytes 1572868
  (73 other events, 212.3 us)
Sparse Core Ops, SparseCore 0:
  9.6 118.0 all-gather.16
  132.5 26.1 all-gather.28
  161.2 27.8 all-gather.30
  190.8 27.8 all-gather.20
  220.5 27.8 all-gather.18
  249.8 45.9 all-gather.22
  297.4 148.3 all-gather.24
  447.3 147.8 all-gather.26
  662.9 69.4 reduce-scatter.8
  736.1 71.2 reduce-scatter.6
  810.3 148.8 reduce-scatter.12
  965.6 154.0 reduce-scatter.10
  1122.7 363.3 reduce-scatter.16
  1488.9 362.1 reduce-scatter.14
where the time goes:
time: 1860 us
  waiting for transfers between devices  1460 us (78%)
  matrix products  130 us (7%)
  blocking collectives  125 us (7%)
  local copies, waits for them, and re-layouts  97.7 us (5%)
  other arithmetic  28.4 us (2%)
    reduce_scatter x1, waiting for transfers between devices, per_device(): lax.psum_scatter(totals[11], ('ctx', 'fsdp'), scatter_dimension=0, tiled=...  366 us
    reduce_scatter x1, waiting for transfers between devices, per_device(): lax.psum_scatter(totals[9], ('ctx', 'fsdp'), scatter_dimension=0, tiled=T...  365 us
    reduce_scatter x1, waiting for transfers between devices, per_device(): lax.psum_scatter(totals[2], ('ctx', 'fsdp'), scatter_dimension=0, tiled=T...  161 us
    all_gather x1, waiting for transfers between devices, per_device(): lax.all_gather(w_up, 'fsdp', axis=0, tiled=True)  146 us
    all_gather x1, waiting for transfers between devices, per_device(): lax.all_gather(w_down, 'fsdp', axis=0, tiled=True)  143 us
    all_gather x1, waiting for transfers between devices, per_device(): lax.all_gather(w_qkv, 'fsdp', axis=0, tiled=True)  96.4 us
    reduce_scatter x2, waiting for transfers between devices, per_device(): lax.psum_scatter(key_terms.reshape(seq_len, 2 * D), 'ctx', scatter_dimens...  86.3 us
    dynamic_update_slice x8, local copies, waits for them, and re-layouts, per_device(): lax.scan(backward_step, jnp.zeros((tokens, HEADS, HEAD_DIM), jnp.float32)...  41 us
  transfers between devices with their start and end apart: 14, of which 12 were waited for; matrix products, arithmetic and copies ran while one was open for 9% of the time, Pallas kernels for 0%

commit v1 on v0

--- a/solution.py
+++ b/solution.py
@@ -67,7 +67,7 @@
     return (probs * (grad_probs - row_delta[:, :, None]) * scale).astype(jnp.bfloat16)
 
 
-def per_device(
+def per_device_ctx(
     layer_in,
     block_order,
     ln1_gain,
@@ -322,6 +322,181 @@
     )
 
 
+def gather_z(item, axis=0):
+    return lax.all_gather(item, "fsdp", axis=axis, tiled=True)
+
+
+def per_device_tp(
+    layer_in,
+    block_order,
+    ln1_gain,
+    ln1_shift,
+    w_qkv,
+    b_query,
+    b_value,
+    w_out,
+    b_out,
+    ln2_gain,
+    ln2_shift,
+    w_up,
+    b_up,
+    w_down,
+    b_down,
+    cotangent,
+):
+    n_ctx = lax.axis_size("ctx")
+    n_z = lax.axis_size("fsdp")
+    mine = lax.axis_index("ctx")
+    seqs, tokens, width = layer_in.shape
+    seq_len = tokens * n_ctx
+    half_rows = tokens // 2
+    ff = w_up.shape[1]
+    hid = ff // (n_ctx * n_z)
+    scale = HEAD_DIM ** (-0.5)
+    f32, bf16 = jnp.float32, jnp.bfloat16
+
+    def pick(item, count):
+        return lax.dynamic_slice_in_dim(item, mine * count, count, axis=0)
+
+    smalls = gather_z(
+        jnp.stack(
+            [ln1_gain, ln1_shift, b_query, b_value, b_out, ln2_gain, ln2_shift, b_down]
+            + [b_up.reshape(n_z, -1)[part] for part in range(n_z)]
+        ),
+        axis=1,
+    ).astype(f32)
+    first_gain, first_shift, query_bias, value_bias, out_bias, second_gain, second_shift, down_bias = (
+        smalls[row] for row in range(8)
+    )
+    up_bias = jnp.transpose(smalls[8:].reshape(n_z, n_z, -1), (1, 0, 2)).reshape(n_z, n_ctx, hid)
+    up_bias = lax.dynamic_index_in_dim(up_bias, mine, axis=1, keepdims=False).reshape(-1)
+    query_bias = pick(query_bias, HEAD_DIM)
+    value_bias = pick(value_bias, HEAD_DIM)
+
+    rows_z = w_qkv.shape[0]
+    qkv_slice = lax.dynamic_index_in_dim(
+        w_qkv.reshape(rows_z, 3, HEADS, HEAD_DIM), mine, axis=2, keepdims=False
+    ).reshape(rows_z, 3 * HEAD_DIM)
+    up_slice = lax.dynamic_index_in_dim(
+        w_up.reshape(rows_z, n_z, n_ctx, hid), mine, axis=2, keepdims=False
+    ).reshape(rows_z, n_z * hid)
+    down_slice = pick(w_down, hid)
+    qkv_w = gather_z(qkv_slice)
+    out_w = gather_z(w_out)
+    up_w = gather_z(up_slice)
+    down_w = gather_z(down_slice)
+
+    inputs = layer_in.astype(f32)
+    first_out, first_normed, first_inv = normalize(inputs, first_gain, first_shift)
+    h1 = lax.all_gather(first_out.astype(bf16), "ctx", axis=1, tiled=True)
+    cot = lax.all_gather(cotangent, "ctx", axis=1, tiled=True)
+    projected = jnp.einsum("std,de->ste", h1, qkv_w, preferred_element_type=f32)
+    query = (projected[..., :HEAD_DIM] + query_bias).astype(bf16)
+    key = projected[..., HEAD_DIM : 2 * HEAD_DIM].astype(bf16)
+    value = (projected[..., 2 * HEAD_DIM :] + value_bias).astype(bf16)
+    pos = jnp.stack([token_positions(block_order[s], seq_len, half_rows) for s in range(seqs)])
+    allowed = pos[:, :, None] >= pos[:, None, :]
+    scores = jnp.einsum("sqd,skd->sqk", query, key, preferred_element_type=f32) * scale
+    scores = jnp.where(allowed, scores, NEG_LARGE)
+    top = jnp.max(scores, axis=-1, keepdims=True)
+    weights = jnp.where(allowed, jnp.exp(scores - top), 0.0)
+    probs = weights / jnp.sum(weights, axis=-1, keepdims=True)
+    probs_low = probs.astype(bf16)
+    attn = jnp.einsum("sqk,skd->sqd", probs_low, value, preferred_element_type=f32).astype(bf16)
+    attn_low = lax.all_to_all(attn, "ctx", split_axis=1, concat_axis=2, tiled=True)
+    resid = inputs + jnp.einsum("std,de->ste", attn_low, out_w, preferred_element_type=f32) + out_bias
+    second_out, second_normed, second_inv = normalize(resid, second_gain, second_shift)
+    h2 = lax.all_gather(second_out.astype(bf16), "ctx", axis=1, tiled=True)
+    hidden = jnp.einsum("std,df->stf", h2, up_w, preferred_element_type=f32) + up_bias
+    active = gelu_tanh(hidden).astype(bf16)
+    down_part = jnp.einsum("stf,fd->std", active, down_w, preferred_element_type=f32)
+    grad_active = jnp.einsum("std,fd->stf", cot, down_w, preferred_element_type=f32)
+    grad_hidden = (grad_active * gelu_slope(hidden)).astype(bf16)
+    second_part = jnp.einsum("stf,df->std", grad_hidden, up_w, preferred_element_type=f32)
+    term_down = jnp.einsum("stf,std->fd", active, cot, preferred_element_type=f32)
+    term_up = jnp.einsum("std,stf->df", h2, grad_hidden, preferred_element_type=f32)
+    down_sum = lax.psum_scatter(down_part, "ctx", scatter_dimension=1, tiled=True)
+    grad_second = lax.psum_scatter(second_part, "ctx", scatter_dimension=1, tiled=True)
+    result = (resid + down_sum + down_bias).astype(bf16)
+    grad_outf = cotangent.astype(f32)
+    grad_resid = grad_outf + normalize_back(grad_second, second_normed, second_inv, second_gain)
+    grad_branch = grad_resid.astype(bf16)
+    term_out = jnp.einsum("std,ste->de", attn_low, grad_branch, preferred_element_type=f32)
+    grad_attn = jnp.einsum("ste,de->std", grad_branch, out_w, preferred_element_type=f32).astype(bf16)
+    dout = lax.all_to_all(grad_attn, "ctx", split_axis=2, concat_axis=1, tiled=True)
+    grad_value = jnp.einsum("sqk,sqd->skd", probs_low, dout, preferred_element_type=f32)
+    grad_probs = jnp.einsum("sqd,skd->sqk", dout, value, preferred_element_type=f32)
+    delta = jnp.sum(probs * grad_probs, axis=-1, keepdims=True)
+    grad_scores = (probs * (grad_probs - delta) * scale).astype(bf16)
+    grad_query = jnp.einsum("sqk,skd->sqd", grad_scores, key, preferred_element_type=f32)
+    grad_key = jnp.einsum("sqk,sqd->skd", grad_scores, query, preferred_element_type=f32)
+    grad_proj = jnp.concatenate([grad_query, grad_key, grad_value], axis=-1).astype(bf16)
+    term_qkv = jnp.einsum("std,ste->de", h1, grad_proj, preferred_element_type=f32)
+    first_part = jnp.einsum("ste,de->std", grad_proj, qkv_w, preferred_element_type=f32)
+    grad_first = lax.psum_scatter(first_part, "ctx", scatter_dimension=1, tiled=True)
+    grad_input = grad_resid + normalize_back(grad_first, first_normed, first_inv, first_gain)
+
+    both = (0, 1)
+    grad_projf = grad_proj.astype(f32)
+    every = jnp.stack(
+        [
+            jnp.sum(grad_first * first_normed, axis=both),
+            jnp.sum(grad_first, axis=both),
+            jnp.sum(grad_branch.astype(f32), axis=both),
+            jnp.sum(grad_second * second_normed, axis=both),
+            jnp.sum(grad_second, axis=both),
+            jnp.sum(grad_outf, axis=both),
+        ]
+    )
+    every = lax.psum_scatter(every, ("ctx", "fsdp"), scatter_dimension=1, tiled=True)
+    sum_query = jnp.sum(grad_projf[..., :HEAD_DIM], axis=both)
+    sum_value = jnp.sum(grad_projf[..., 2 * HEAD_DIM :], axis=both)
+    own = lax.psum_scatter(
+        jnp.stack([sum_query, sum_value]), "fsdp", scatter_dimension=1, tiled=True
+    )
+
+    def to_owner(block):
+        moves = []
+        for col in range(n_ctx):
+            for layer in range(n_z):
+                place = layer * n_ctx + col
+                moves.append((col * n_z + layer, place))
+        return lax.ppermute(block, ("ctx", "fsdp"), moves)
+
+    grad_down = to_owner(lax.psum_scatter(term_down, "fsdp", scatter_dimension=0, tiled=True))
+    up_sum = jnp.sum(grad_hidden.astype(f32), axis=both)
+    grad_up_bias = to_owner(lax.psum_scatter(up_sum, "fsdp", scatter_dimension=0, tiled=True))
+
+    def rows_to_owner(term, groups):
+        cols = term.shape[1]
+        part = term.reshape(n_ctx, n_z, -1, cols)
+        part = lax.psum_scatter(part, "fsdp", scatter_dimension=1, tiled=True)[:, 0]
+        part = lax.all_to_all(part, "ctx", split_axis=0, concat_axis=0, tiled=True)
+        part = part.reshape(n_ctx, -1, groups, cols // groups)
+        return jnp.transpose(part, (1, 2, 0, 3)).reshape(part.shape[1], n_ctx * cols)
+
+    grad_up = rows_to_owner(term_up, n_z)
+    grad_qkv = rows_to_owner(term_qkv, 3)
+    grad_out_w = lax.psum_scatter(term_out, ("ctx", "fsdp"), scatter_dimension=0, tiled=True)
+    return (
+        result,
+        grad_input.astype(bf16),
+        every[0],
+        every[1],
+        grad_qkv,
+        own[0],
+        own[1],
+        grad_out_w,
+        every[2],
+        every[3],
+        every[4],
+        grad_up,
+        grad_up_bias,
+        grad_down,
+        every[5],
+    )
+
+
 def solution(mesh):
     placed = (
         P("fsdp", "ctx", None),
@@ -341,8 +516,9 @@
         P("fsdp"),
         P("fsdp", "ctx", None),
     )
+    by_heads = mesh.shape["ctx"] == HEADS
     return jax.shard_map(
-        per_device,
+        per_device_tp if by_heads else per_device_ctx,
         mesh=mesh,
         in_specs=placed,
         out_specs=(

time: 1860 us -> 1060 us (0.57)
  waiting for transfers between devices: 1460 us -> 762 us
  blocking collectives: 125 us -> 56.4 us
  local copies, waits for them, and re-layouts: 97.7 us -> 47.1 us
  starting transfers between devices: 0.77 us -> 28.5 us
    reduce_scatter x6, waiting for transfers between devices: 1020 us -> 407 us  [the longest x1 142 us: per_device_tp(): lax.psum_scatter(term_out, ('ctx', 'fsdp'), scatter_dimension=0, tiled=True)]
    all_gather x8 -> x6, waiting for transfers between devices: 437 us -> 145 us  [the longest x3 53.2 us: gather_z(): return lax.all_gather(item, 'fsdp', axis=axis, tiled=True)]
    unnamed x14 -> x18, waiting for transfers between devices: 3.27 us -> 211 us
    all_gather x9 -> x2, blocking collectives: 86.2 us -> 32.5 us  [gather_z(): return lax.all_gather(item, 'fsdp', axis=axis, tiled=True)]
    dynamic_update_slice x8 -> x0, local copies, waits for them, and re-layouts: 41 us -> none  [per_device(): lax.scan(backward_step, jnp.zeros((tokens, HEADS, HEAD_DIM), jnp.float32)...]
    unnamed x1, blocking collectives: 38.9 us -> 11.3 us
    dot_general x60 -> x17, matrix products: 130 us -> 115 us  [the longest x1 14.8 us: per_device_tp(): jnp.einsum('sqk,skd->sqd', grad_scores, key, preferred_element_type=f32)]
  transfers between devices with their start and end apart: 14 -> 20, of which waited for: 12 -> 15; matrix products, arithmetic and copies ran while one was open for 9% -> 10% of each run, Pallas kernels for 0% -> 0%
where the time goes in v1:
time: 1060 us; the launch traced here: 1050 us
  waiting for transfers between devices  762 us (72%)
  matrix products  123 us (12%)
  blocking collectives  56.4 us (5%)
  local copies, waits for them, and re-layouts  47.1 us (4%)
  starting transfers between devices  28.5 us (3%)
  other arithmetic  18.4 us (2%)
  between operations  15.3 us (1%)
    unnamed x18, waiting for transfers between devices  211 us
    reduce_scatter x1, waiting for transfers between devices, per_device_tp(): lax.psum_scatter(term_out, ('ctx', 'fsdp'), scatter_dimension=0, tiled=True)  142 us
    reduce_scatter x1, waiting for transfers between devices, per_device_tp(): lax.psum_scatter(down_part, 'ctx', scatter_dimension=1, tiled=True)  73.4 us
    reduce_scatter x1, waiting for transfers between devices, per_device_tp(): lax.psum_scatter(second_part, 'ctx', scatter_dimension=1, tiled=True)  60.9 us
    all_gather x3, waiting for transfers between devices, gather_z(): return lax.all_gather(item, 'fsdp', axis=axis, tiled=True)  53.2 us
    reduce_scatter x1, waiting for transfers between devices, rows_to_owner(): part = lax.psum_scatter(part, 'fsdp', scatter_dimension=1, tiled=True)[:, 0]  45.8 us
    reduce_scatter x1, waiting for transfers between devices, per_device_tp(): lax.psum_scatter(first_part, 'ctx', scatter_dimension=1, tiled=True)  45.3 us
    reduce_scatter x1, waiting for transfers between devices, per_device_tp(): lax.psum_scatter(term_down, 'fsdp', scatter_dimension=0, tiled=True)  39 us
  transfers between devices with their start and end apart: 20, of which 15 were waited for; matrix products, arithmetic and copies ran while one was open for 10% of the time, Pallas kernels for 0%

profile of v1, /device:TPU:0, one launch (start us, length us, event | category | flops | bytes accessed | tf_op | source)
XLA Modules:
  0.0 1050.8 jit_solution(957857499054609545)
XLA Ops:
  16.1 14.8 %all_gather.24 = bf16[12,1024]{1,0:T(8,128)(2,1)S(1)} all-gather(bf16[12,256]{1,0:T(8,128)(2,1)S(1)} %stack.71), channel_id=1, replica_groups=mesh['ctx'=8,'fsdp'=4] {'fsdp'}, dimensions={1}, use_global_device_ids=true | all-gather | bytes 30720 | tf_op jit(solution)/shard_map/all_gather | solution.py:326
  30.9 2.1 fusion.58
  34.7 2.6 copy.117
  38.5 17.7 %all_gather.26 = bf16[1024,384]{1,0:T(8,128)(2,1)S(1)} all-gather(bf16[256,384]{1,0:T(8,128)(2,1)S(1)} %copy.118), channel_id=1, replica_groups=mesh['ctx'=8,'fsdp'=4] {'fsdp'}, dimensions={0}, use_global_device_ids=true | all-gather | bytes 983040 | tf_op jit(solution)/shard_map/all_gather | solution.py:326
  56.2 14.8 %all-gather.7.cloned.1.call-done = bf16[2,1024,1024]{2,1,0:T(8,128)(2,1)} async-done(((bf16[2,128,1024]{2,1,0:T(8,128)(2,1)}), bf16[2,1024,1024]{2,1,0:T(8,128)(2,1)}) %all-gather.7.cloned.1.call-update) | async-done | bytes 4194320 | tf_op jit(solution)/shard_map/all_gather | solution.py:391
  71.0 6.2 fusion.79
  77.1 7.3 fusion.105
  84.5 5.4 fusion.36
  91.2 3.5 all-to-all-start
  94.7 2.1 copy.170
  99.3 11.1 %all-gather.11.cloned.1.call-start = ((), (), s32[]{:S(2)}) async-start(), calls=%async_computation.14 | async-start | bytes 4718592 | tf_op jit(solution)/shard_map/all_gather | solution.py:409
  111.8 6.7 all-gather.9.cloned.1.call-done
  118.5 2.6 fusion.106
  124.0 23.3 %all-gather.13.cloned.1.call-done = bf16[1024,512]{1,0:T(8,128)(2,1)} async-done(((bf16[256,512]{1,0:T(8,128)(2,1)}), bf16[1024,512]{1,0:T(8,128)(2,1)}) %all-gather.13.cloned.1.call-update) | async-done | bytes 1048592 | tf_op jit(solution)/shard_map/all_gather | solution.py:326
  147.3 38.6 %all-gather.11.cloned.1.call-done = bf16[2,1024,1024]{2,1,0:T(8,128)(2,1)} async-done(((bf16[2,128,1024]{2,1,0:T(8,128)(2,1)}), bf16[2,1024,1024]{2,1,0:T(8,128)(2,1)}) %all-gather.11.cloned.1.call-update) | async-done | bytes 4194320 | tf_op jit(solution)/shard_map/all_gather | solution.py:409
  185.9 6.9 fusion.73
  192.8 23.1 %all-gather.15.cloned.1.call-done = bf16[512,1024]{1,0:T(8,128)(2,1)} async-done(((bf16[128,1024]{1,0:T(8,128)(2,1)}), bf16[512,1024]{1,0:T(8,128)(2,1)}) %all-gather.15.cloned.1.call-update) | async-done | bytes 1048592 | tf_op jit(solution)/shard_map/all_gather | solution.py:326
  215.9 38.0 %all-gather.17.cloned.1.call-done = bf16[2,1024,1024]{2,1,0:T(8,128)(2,1)} async-done(((bf16[2,128,1024]{2,1,0:T(8,128)(2,1)}), bf16[2,1024,1024]{2,1,0:T(8,128)(2,1)}) %all-gather.17.cloned.1.call-update) | async-done | bytes 4194320 | tf_op jit(solution)/shard_map/all_gather | solution.py:392
  253.9 9.4 convert_reduce_fusion
  263.2 5.6 fusion.71
  270.1 9.2 fusion.69
  279.4 60.9 %reduce-scatter.18.cloned.1.call-done = f32[2,128,1024]{2,1,0:T(8,128)} async-done(((f32[2,1024,1024]{2,1,0:T(8,128)}), f32[2,128,1024]{2,1,0:T(8,128)}) %reduce-scatter.18.cloned.1.call-update) | async-done | bytes 1048592 | tf_op jit(solution)/shard_map/reduce_scatter | solution.py:419
  342.0 73.4 %reduce-scatter.16.cloned.1.call-done = f32[2,128,1024]{2,1,0:T(8,128)} async-done(((f32[2,1024,1024]{2,1,0:T(8,128)}), f32[2,128,1024]{2,1,0:T(8,128)}) %reduce-scatter.16.cloned.1.call-update) | async-done | bytes 1048592 | tf_op jit(solution)/shard_map/reduce_scatter | solution.py:418
  415.4 3.3 convert_reduce_fusion.3
  421.6 12.7 %all_to_all.46 = bf16[2,128,1024]{1,0,2:T(2,128)(2,1)S(1)} all-to-all(bf16[2,128,1024]{1,0,2:T(2,128)(2,1)S(1)} %copy.124), channel_id=1, replica_groups=mesh['ctx'=8,'fsdp'=4] {'ctx'}, dimensions={2} | all-to-all | bytes 1048576 | tf_op jit(solution)/shard_map/all_to_all | solution.py:426
  434.8 4.9 fusion.39
  439.7 5.9 fusion.81
  445.6 14.2 %fusion.48 = bf16[2,1024,128]{1,2,0:T(8,128)(2,1)S(1)} fusion(f32[2,1024,1024]{1,2,0:T(8,128)} %fusion.81, f32[2,1024,1024]{1,2,0:T(8,128)} %get-tuple-element.54, f32[2,1024]{1,0:T(2,128)S(1)} %get-tuple-element.53, f32[2,1024,384]{2,1,0:T(8,128)} %fusion.79, f32[128]{0:T(128)S(1)} %get-tuple-element.59), kind=kOutput, calls=%fused_computation.47 | convolution fusion | flops 552340480 | bytes 35144192 | tf_op jit(solution)/shard_map/sqk,sqd->skd/dot_general | solution.py:432
  459.9 14.8 %fusion.45 = bf16[2,1024,128]{1,2,0:T(8,128)(2,1)} fusion(f32[2,1024,1024]{1,2,0:T(8,128)} %fusion.81, f32[2,1024,384]{2,1,0:T(8,128)} %fusion.79, f32[2,1024,1024]{1,2,0:T(8,128)} %get-tuple-element.54, f32[2,1024]{1,0:T(2,128)S(1)} %get-tuple-element.53), kind=kOutput, calls=%fused_computation.46 | convolution fusion | flops 551816192 | bytes 34619392 | tf_op jit(solution)/shard_map/sqk,skd->sqd/dot_general | solution.py:431
  474.6 6.7 fusion.77
  482.9 5.9 fusion.111
  489.0 9.0 convolution_bitcast_fusion.1
  498.1 4.6 fusion.100
  506.6 45.3 %reduce-scatter.20.cloned.1.call-done = f32[2,128,1024]{2,1,0:T(8,128)} async-done(((f32[2,1024,1024]{2,1,0:T(8,128)}), f32[2,128,1024]{2,1,0:T(8,128)}) %reduce-scatter.20.cloned.1.call-update) | async-done | bytes 1048592 | tf_op jit(solution)/shard_map/reduce_scatter | solution.py:436
  551.9 2.3 fusion.64
  555.3 2.7 convolution_bitcast_fusion
  558.6 82.1 %all-reduce.4.cloned.1.call-done = f32[8,4,32,512]{3,2,1,0:T(8,128)} async-done(((f32[8,4,32,512]{3,2,1,0:T(8,128)}), f32[8,4,32,512]{3,2,1,0:T(8,128)}) %all-reduce.4.cloned.1.call-update) | async-done | bytes 2097168
  640.7 2.5 dynamic-slice_bitcast_fusion
  643.2 3.7 all-to-all-start.3
  646.9 39.0 %reduce-scatter.26.cloned.1.call-done = f32[128,1024]{1,0:T(8,128)} async-done(((f32[512,1024]{1,0:T(8,128)}), f32[128,1024]{1,0:T(8,128)}) %reduce-scatter.26.cloned.1.call-update) | async-done | bytes 524304 | tf_op jit(solution)/shard_map/reduce_scatter | solution.py:466
  685.9 5.3 collective-permute-start.1
  691.2 45.8 %reduce-scatter.22.cloned.1.call-done = f32[8,1,32,384]{3,2,0,1:T(8,128)} async-done(((f32[8,4,32,384]{3,2,0,1:T(8,128)}), f32[8,1,32,384]{3,2,0,1:T(8,128)}) %reduce-scatter.22.cloned.1.call-update) | async-done | bytes 393232 | tf_op jit(solution)/shard_map/reduce_scatter | solution.py:473
  737.0 3.5 all-to-all-start.2
  741.1 11.3 %all-reduce.1 = f32[512]{0:T(512)S(1)} all-reduce(f32[512]{0:T(512)S(1)} %copy-done.15), channel_id=10, replica_groups=mesh['ctx'=8,'fsdp'=4] {'fsdp'}, use_global_device_ids=true, to_apply=%region_30.31.clone | all-reduce | flops 512 | bytes 4096
  756.7 3.7 reduce-scatter.30.cloned.1.call-done
  768.2 2.6 fusion.63
  770.8 123.9 %reduce-scatter.28.cloned.1.call-done = f32[32,6]{1,0:T(8,128)} async-done(((f32[1024,6]{1,0:T(8,128)}), f32[32,6]{1,0:T(8,128)}) %reduce-scatter.28.cloned.1.call-update) | async-done | bytes 784
  899.3 142.4 %reduce-scatter.24.cloned.1.call-done = f32[32,1024]{1,0:T(8,128)} async-done(((f32[1024,1024]{1,0:T(8,128)}), f32[32,1024]{1,0:T(8,128)}) %reduce-scatter.24.cloned.1.call-update) | async-done | bytes 131088 | tf_op jit(solution)/shard_map/reduce_scatter | solution.py:480
  (154 shorter events, 52.3 us)
Async XLA Ops:
  7.2 115.4 %copy-start = (bf16[1024,1024]{1,0:T(8,128)(2,1)S(1)}, bf16[1024,1024]{1,0:T(8,128)(2,1)}, u32[]{:S(2)}) copy-start(bf16[1024,1024]{1,0:T(8,128)(2,1)} %param.29) | copy-start | bytes 6291460
  7.2 63.8 %all-gather.7.cloned.1.call-start = ((), (), s32[]{:S(2)}) async-start(), calls=%async_computation.12 | async-start | bytes 4718592 | tf_op jit(solution)/shard_map/all_gather | solution.py:391
  33.1 85.4 %all-gather.9.cloned.1.call-start = ((), (), s32[]{:S(2)}) async-start(), calls=%async_computation.13 | async-start | bytes 2621440 | tf_op jit(solution)/shard_map/all_gather | solution.py:326
  56.2 21.0 %copy-start.4 = (bf16[1024,384]{1,0:T(8,128)(2,1)}, bf16[1024,384]{1,0:T(8,128)(2,1)S(1)}, u32[]{:S(2)}) copy-start(bf16[1024,384]{1,0:T(8,128)(2,1)S(1)} %all_gather.26) | copy-start | bytes 2359300
  91.2 19.2 %all-to-all-start = ((bf16[2,1024,128]{2,0,1:T(2,128)(2,1)}), bf16[2,1024,128]{2,0,1:T(2,128)(2,1)S(1)}, u32[]{:S(2)}, u32[]{:S(2)}) async-start(bf16[2,1024,128]{2,0,1:T(2,128)(2,1)} %copy.120), calls=%async_computation | async-start | bytes 1048576 | tf_op jit(solution)/shard_map/all_to_all | solution.py:406
  94.7 52.6 %all-gather.13.cloned.1.call-start = ((), (), s32[]{:S(2)}) async-start(), calls=%async_computation.15 | async-start | bytes 1310720 | tf_op jit(solution)/shard_map/all_gather | solution.py:326
  99.3 86.6 %all-gather.11.cloned.1.call-start = ((), (), s32[]{:S(2)}) async-start(), calls=%async_computation.14 | async-start | bytes 4718592 | tf_op jit(solution)/shard_map/all_gather | solution.py:409
  121.1 219.2 %copy-start.2 = (f32[2,128,1024]{2,1,0:T(8,128)}, f32[2,128,1024]{2,1,0:T(8,128)S(1)}, u32[]{:S(2)}) copy-start(f32[2,128,1024]{2,1,0:T(8,128)S(1)} %get-tuple-element.56) | copy-start | bytes 3145732
  122.5 93.4 %all-gather.15.cloned.1.call-start = ((), (), s32[]{:S(2)}) async-start(), calls=%async_computation.16 | async-start | bytes 1310720 | tf_op jit(solution)/shard_map/all_gather | solution.py:326
  123.3 130.6 %all-gather.17.cloned.1.call-start = ((), (), s32[]{:S(2)}) async-start(), calls=%async_computation.18 | async-start | bytes 4718592 | tf_op jit(solution)/shard_map/all_gather | solution.py:392
  123.9 216.4 %reduce-scatter.18.cloned.1.call-start = ((), (), s32[]{:S(2)}) async-start(), calls=%async_computation.19 | async-start | bytes 9437184 | tf_op jit(solution)/shard_map/reduce_scatter | solution.py:419
  253.9 9.4 copy-start.16
  263.2 5.6 copy-start.7
  268.8 1.2 copy-start.17
  268.9 146.6 %reduce-scatter.16.cloned.1.call-start = ((), (), s32[]{:S(2)}) async-start(), calls=%async_computation.17 | async-start | bytes 9437184 | tf_op jit(solution)/shard_map/reduce_scatter | solution.py:418
  279.3 139.5 %copy-start.6 = (bf16[1024,1024]{1,0:T(8,128)(2,1)S(1)}, bf16[1024,1024]{1,0:T(8,128)(2,1)}, u32[]{:S(2)}) copy-start(bf16[1024,1024]{1,0:T(8,128)(2,1)} %all-gather.9.cloned.1.call-done) | copy-start | bytes 6291460
  279.3 272.5 %reduce-scatter.20.cloned.1.call-start = ((), (), s32[]{:S(2)}) async-start(), calls=%async_computation.20 | async-start | bytes 9437184 | tf_op jit(solution)/shard_map/reduce_scatter | solution.py:436
  439.7 34.9 %copy-start.10 = (bf16[2,1024,128]{1,2,0:T(8,128)(2,1)}, bf16[2,1024,128]{1,2,0:T(8,128)(2,1)S(1)}, u32[]{:S(2)}) copy-start(bf16[2,1024,128]{1,2,0:T(8,128)(2,1)S(1)} %fusion.39) | copy-start | bytes 1572868
  459.8 14.8 %copy-start.12 = (bf16[2,1024,128]{1,2,0:T(8,128)(2,1)}, bf16[2,1024,128]{1,2,0:T(8,128)(2,1)S(1)}, u32[]{:S(2)}) copy-start(bf16[2,1024,128]{1,2,0:T(8,128)(2,1)S(1)} %fusion.48) | copy-start | bytes 1572868
  459.9 14.8 %copy-start.5 = (bf16[1024,384]{1,0:T(8,128)(2,1)S(1)}, bf16[1024,384]{1,0:T(8,128)(2,1)}, u32[]{:S(2)}) copy-start(bf16[1024,384]{1,0:T(8,128)(2,1)} %copy-done.4) | copy-start | bytes 2359300
  481.3 1.6 copy-start.8
  481.3 159.4 %all-reduce.4.cloned.1.call-start = ((), (), s32[]{:S(2)}) async-start(), calls=%async_computation.26 | async-start | bytes 4194304
  488.9 9.2 copy-start.11
  488.9 9.2 copy-start.13
  488.9 9.2 copy-start.14
  488.9 197.0 %reduce-scatter.26.cloned.1.call-start = ((), (), s32[]{:S(2)}) async-start(), calls=%async_computation.23 | async-start | bytes 2621440 | tf_op jit(solution)/shard_map/reduce_scatter | solution.py:466
  498.0 238.9 %reduce-scatter.22.cloned.1.call-start = ((), (), s32[]{:S(2)}) async-start(), calls=%async_computation.21 | async-start | bytes 1966080 | tf_op jit(solution)/shard_map/reduce_scatter | solution.py:473
  504.0 47.9 %copy-start.3 = (bf16[2,128,1024]{2,1,0:T(8,128)(2,1)S(1)}, bf16[2,128,1024]{2,1,0:T(8,128)(2,1)}, u32[]{:S(2)}) copy-start(bf16[2,128,1024]{2,1,0:T(8,128)(2,1)} %param.16) | copy-start | bytes 1572868
  504.0 51.3 %copy-start.9 = (bf16[2,128,1024]{2,1,0:T(8,128)(2,1)S(1)}, bf16[2,128,1024]{2,1,0:T(8,128)(2,1)}, u32[]{:S(2)}) copy-start(bf16[2,128,1024]{2,1,0:T(8,128)(2,1)} %all_to_all.35) | copy-start | bytes 1572868
  504.0 256.4 %reduce-scatter.30.cloned.1.call-start = ((), (), s32[]{:S(2)}) async-start(), calls=%async_computation.25 | async-start | bytes 81920
  506.5 388.2 %reduce-scatter.28.cloned.1.call-start = ((), (), s32[]{:S(2)}) async-start(), calls=%async_computation.24 | async-start | bytes 540672
  555.3 2.8 copy-start.20
  555.3 486.4 %reduce-scatter.24.cloned.1.call-start = ((), (), s32[]{:S(2)}) async-start(), calls=%async_computation.22 | async-start | bytes 4325376 | tf_op jit(solution)/shard_map/reduce_scatter | solution.py:480
  558.0 183.1 %copy-start.15 = (f32[512]{0:T(512)S(1)}, f32[512]{0:T(512)}, u32[]{:S(2)}) copy-start(f32[512]{0:T(512)} %get-tuple-element.57) | copy-start | bytes 6148
  643.2 48.0 %all-to-all-start.3 = ((f32[8,32,512]{2,1,0:T(8,128)}), f32[8,32,512]{2,1,0:T(8,128)S(1)}, u32[]{:S(2)}, u32[]{:S(2)}) async-start(f32[8,32,512]{2,1,0:T(8,128)} %dynamic-slice_bitcast_fusion), calls=%async_computation.8 | async-start | bytes 1048576 | tf_op jit(solution)/shard_map/all_to_all | solution.py:474
  685.9 70.8 %collective-permute-start.1 = (f32[128,1024]{1,0:T(8,128)}, f32[128,1024]{1,0:T(8,128)}, u32[]{:S(2)}, u32[]{:S(2)}) collective-permute-start(f32[128,1024]{1,0:T(8,128)} %reduce-scatter.26.cloned.1.call-done), channel_id=1, source_target_pairs={{0,0},{1,8},{2,16},{3,24},{4,1},{5,9},{6,17},{7,25},{8,2},{9,10},{... | collective-permute-start | bytes 1572872 | tf_op jit(solution)/shard_map/ppermute | solution.py:464
  737.0 27.5 %all-to-all-start.2 = ((f32[8,32,384]{2,1,0:T(8,128)}), f32[8,32,384]{2,1,0:T(8,128)S(1)}, u32[]{:S(2)}, u32[]{:S(2)}) async-start(f32[8,32,384]{2,1,0:T(8,128)} %bitcast.155), calls=%async_computation.6 | async-start | bytes 786432 | tf_op jit(solution)/shard_map/all_to_all | solution.py:474
  752.4 0.7 collective-permute-start
  753.1 1.0 copy-start.18
  754.1 290.0 %copy-start.1 = (bf16[1024,1024]{1,0:T(8,128)(2,1)S(1)}, bf16[1024,1024]{1,0:T(8,128)(2,1)}, u32[]{:S(2)}) copy-start(bf16[1024,1024]{1,0:T(8,128)(2,1)} %param.29) | copy-start | bytes 6291460
  765.4 276.3 %copy-start.19 = (f32[128]{0:T(128)S(1)}, f32[128]{0:T(128)}, u32[]{:S(2)}) copy-start(f32[128]{0:T(128)} %copy-done.18) | copy-start | bytes 1540
Sparse Core Ops, SparseCore 0:
  33.2 37.7 all-gather.6
  72.5 45.9 all-gather.8
  120.6 26.6 all-gather.12
  149.7 36.1 all-gather.10
  187.9 27.9 all-gather.14
  217.6 36.1 all-gather.16
  269.0 71.2 reduce-scatter.17
  344.1 71.2 reduce-scatter.15
  481.5 70.3 reduce-scatter.19
  554.2 86.4 all-reduce.3
  643.0 42.8 reduce-scatter.25
  688.1 48.7 reduce-scatter.21
  739.9 20.4 reduce-scatter.29
  762.5 132.2 reduce-scatter.27
  897.6 144.0 reduce-scatter.23

commit v2 on v0

--- a/solution.py
+++ b/solution.py
@@ -1,8 +1,11 @@
 import math
+import types
 
 import jax
 import jax.numpy as jnp
 from jax import lax
+from jax.experimental import pallas as pl
+from jax.experimental.pallas import tpu as pltpu
 from jax.sharding import PartitionSpec as P
 
 D = 1024
@@ -14,6 +17,7 @@
 NEG_LARGE = -1e30
 GELU_C = math.sqrt(2.0 / math.pi)
 GELU_K = 0.044715
+VMEM_BYTES = 63 << 20
 
 
 def gelu_tanh(values):
@@ -67,7 +71,7 @@
     return (probs * (grad_probs - row_delta[:, :, None]) * scale).astype(jnp.bfloat16)
 
 
-def per_device(
+def per_device_ctx(
     layer_in,
     block_order,
     ln1_gain,
@@ -322,6 +326,957 @@
     )
 
 
+LOG2E = 1.4426950408889634
+HOPS = 3
+SMALL_ROWS = 16
+
+
+def dot_as(left, right, left_dim, right_dim):
+    return lax.dot_general(
+        left, right, (((left_dim,), (right_dim,)), ((), ())), preferred_element_type=jnp.float32
+    )
+
+
+def dot_nn(left, right):
+    return dot_as(left, right, 1, 0)
+
+
+def dot_nt(left, right):
+    return dot_as(left, right, 1, 1)
+
+
+def dot_tn(left, right):
+    return dot_as(left, right, 0, 0)
+
+
+class Ring:
+    def __init__(self):
+        self.col = lax.axis_index("ctx")
+        self.layer = lax.axis_index("fsdp")
+        col = self.col
+        self.sib = col + 1 - 2 * (col % 2)
+        self.xnb = col + 2 - 4 * ((col // 2) % 2)
+        self.ynb = col + 4 - 8 * (col // 4)
+        self.diag = self.xnb + self.ynb - col
+        self.xsib = self.xnb + self.sib - col
+        self.ysib = self.ynb + self.sib - col
+        self.dsib = self.diag + self.sib - col
+
+    def flat(self, col):
+        return (col, self.layer)
+
+    def up(self, hop):
+        return (self.layer + hop) % 4
+
+
+def send(src, dst, send_sem, recv_sem, where):
+    copy = pltpu.make_async_remote_copy(
+        src_ref=src,
+        dst_ref=dst,
+        send_sem=send_sem,
+        recv_sem=recv_sem,
+        device_id=where,
+        device_id_type=pl.DeviceIdType.MESH,
+    )
+    copy.start()
+    return copy
+
+
+def move(src, dst, sem):
+    copy = pltpu.make_async_copy(src, dst, sem)
+    copy.start()
+    return copy
+
+
+class Gather:
+    def __init__(self, ring, block, half, ssem, rsem):
+        self.ring, self.block, self.half = ring, block, half
+        self.ssem, self.rsem = ssem, rsem
+        self.open = []
+
+    def go(self, ref, slot_s, slot_r, col):
+        copy = send(ref, ref, self.ssem.at[slot_s], self.rsem.at[slot_r], self.ring.flat(col))
+        self.open.append(copy)
+        return copy
+
+    def start(self):
+        ring = self.ring
+        own = self.block(ring.col)
+        self.by_x = self.go(own, 0, 0, ring.xnb)
+        self.by_y = self.go(own, 1, 1, ring.ynb)
+        self.by_sib = self.go(own, 2, 2, ring.sib)
+
+    def relay(self):
+        ring = self.ring
+        self.by_x.wait_recv()
+        self.diag_y = self.go(self.half(ring.xnb, 0), 3, 3, ring.ynb)
+        self.x_sib = self.go(self.block(ring.xnb), 4, 4, ring.sib)
+        self.by_y.wait_recv()
+        self.diag_x = self.go(self.half(ring.ynb, 1), 5, 5, ring.xnb)
+        self.y_sib = self.go(self.block(ring.ynb), 6, 6, ring.sib)
+
+    def relay_diag(self):
+        ring = self.ring
+        self.diag_y.wait_recv()
+        self.diag_x.wait_recv()
+        self.d_sib = self.go(self.block(ring.diag), 7, 7, ring.sib)
+
+    def finish(self):
+        self.by_sib.wait_recv()
+        self.x_sib.wait_recv()
+        self.y_sib.wait_recv()
+        self.d_sib.wait_recv()
+
+    def drain(self):
+        for copy in self.open:
+            copy.wait_send()
+
+
+class Scatter:
+    def __init__(self, ring, part, rows, from_sib, from_diag, from_side, ssem, rsem):
+        self.ring, self.part, self.rows = ring, part, rows
+        self.from_sib, self.from_diag, self.from_side = from_sib, from_diag, from_side
+        self.ssem, self.rsem = ssem, rsem
+        self.open = []
+
+    def at(self, col, first=0, count=None):
+        count = self.rows if count is None else count
+        return pl.ds(pl.multiple_of(col * self.rows + first, count), count)
+
+    def go(self, src, dst, slot, col):
+        copy = send(src, dst, self.ssem.at[slot], self.rsem.at[slot], self.ring.flat(col))
+        self.open.append(copy)
+        return copy
+
+    def start(self):
+        ring = self.ring
+        self.chip = {}
+        for slot, col in ((3, ring.dsib), (1, ring.xsib), (2, ring.ysib), (0, ring.sib)):
+            self.chip[slot] = self.go(
+                self.part.at[self.at(col)], self.from_sib.at[slot], slot, ring.sib
+            )
+
+    def add(self, col, extra, first=0, count=None):
+        where = self.at(col, first, count)
+        total = self.part[where].astype(jnp.float32)
+        for item in extra:
+            total = total + item.astype(jnp.float32)
+        self.part[where] = total.astype(jnp.bfloat16)
+
+    def middle(self):
+        ring = self.ring
+        half = self.rows // 2
+        self.chip[3].wait_recv()
+        self.add(ring.diag, [self.from_sib[3]])
+        self.diag_x = self.go(
+            self.part.at[self.at(ring.diag, 0, half)], self.from_diag.at[0], 4, ring.xnb
+        )
+        self.diag_y = self.go(
+            self.part.at[self.at(ring.diag, half, half)], self.from_diag.at[1], 5, ring.ynb
+        )
+
+    def last(self):
+        ring = self.ring
+        half = self.rows // 2
+        self.chip[1].wait_recv()
+        self.chip[2].wait_recv()
+        self.diag_x.wait_recv()
+        self.add(ring.ynb, [self.from_sib[2, :half], self.from_diag[0]], 0, half)
+        self.add(ring.ynb, [self.from_sib[2, half:]], half, half)
+        self.side_y = self.go(self.part.at[self.at(ring.ynb)], self.from_side.at[1], 7, ring.ynb)
+        self.diag_y.wait_recv()
+        self.add(ring.xnb, [self.from_sib[1, :half]], 0, half)
+        self.add(ring.xnb, [self.from_sib[1, half:], self.from_diag[1]], half, half)
+        self.side_x = self.go(self.part.at[self.at(ring.xnb)], self.from_side.at[0], 6, ring.xnb)
+
+    def finish(self):
+        self.chip[0].wait_recv()
+        self.side_y.wait_recv()
+        self.side_x.wait_recv()
+        total = self.part[self.at(self.ring.col)].astype(jnp.float32)
+        total = total + self.from_sib[0].astype(jnp.float32)
+        return (
+            total + self.from_side[0].astype(jnp.float32) + self.from_side[1].astype(jnp.float32)
+        )
+
+    def drain(self):
+        for copy in self.open:
+            copy.wait_send()
+
+
+def row_norm(values):
+    average = jnp.mean(values, axis=-1, keepdims=True)
+    centered = values - average
+    inv_dev = lax.rsqrt(jnp.mean(centered * centered, axis=-1, keepdims=True) + EPSILON)
+    return centered * inv_dev, inv_dev
+
+
+def layer_kernel(scale, refs):
+    f32, bf16 = jnp.float32, jnp.bfloat16
+    ring = Ring()
+    col, layer = ring.col, ring.layer
+    seqs, tokens, width = refs.x.shape
+    seq_len = tokens * 8
+    head = HEAD_DIM
+    rows_z = width // 4
+    hid = refs.wu.shape[1] // 4
+    step_c2 = scale * LOG2E
+    R = refs
+    mine = pl.ds(pl.multiple_of(col * tokens, tokens), tokens)
+    head_cols = pl.multiple_of(col * head, head)
+
+    barrier = pltpu.get_barrier_semaphore()
+    me = col * 4 + layer
+    for hop in range(1, 32):
+        other = (me + hop) % 32
+        pl.semaphore_signal(
+            barrier, 1, device_id=(other // 4, other % 4), device_id_type=pl.DeviceIdType.MESH
+        )
+    local = R.lsem
+    load_x = move(R.x, R.xb, local.at[0])
+    load_ct = [move(R.cot.at[s], R.ct.at[s, mine], local.at[1 + s]) for s in range(seqs)]
+    qkv_rows = pl.ds(pl.multiple_of(layer * rows_z, rows_z), rows_z)
+    load_q = []
+    for g in range(3):
+        src = R.w_qkv.at[:, pl.ds(pl.multiple_of(g * width + col * head, head), head)]
+        load_q.append(move(src, R.wq.at[qkv_rows, g * head : (g + 1) * head], local.at[3 + g]))
+    small_rows = 32
+    out_src = R.w_out.at[pl.ds(pl.multiple_of(col * small_rows, small_rows), small_rows)]
+    load_o = move(out_src, R.wo.at[layer, col], local.at[6])
+    load_u = []
+    for g in range(4):
+        src = R.w_up.at[:, pl.ds(pl.multiple_of(g * width + col * hid, hid), hid)]
+        load_u.append(move(src, R.wu.at[qkv_rows, g * hid : (g + 1) * hid], local.at[7 + g]))
+    down_src = R.w_down.at[pl.ds(pl.multiple_of(col * hid, hid), hid)]
+    down_rows = pl.ds(pl.multiple_of(layer * hid, hid), hid)
+    load_d = move(down_src, R.wd.at[down_rows], local.at[11])
+    R.par[layer] = R.params[...]
+    pl.semaphore_wait(barrier, 31)
+
+    zs, zr = R.zs, R.zr
+
+    def to_planes(src, dst, slot):
+        return [
+            send(src, dst, zs.at[slot, hop - 1], zr.at[slot, hop - 1], (col, ring.up(hop)))
+            for hop in range(1, 4)
+        ]
+
+    send_par = to_planes(R.params, R.par.at[layer], 0)
+    send_q = []
+    for g in range(3):
+        src = R.w_qkv.at[:, pl.ds(pl.multiple_of(g * width + col * head, head), head)]
+        send_q += to_planes(src, R.wq.at[qkv_rows, g * head : (g + 1) * head], 1 + g)
+
+    def gather_rows(ref, s, slot):
+
+        def block(index):
+            return ref.at[s, pl.ds(pl.multiple_of(index * tokens, tokens), tokens)]
+
+        def half(index, part):
+            count = tokens // 2
+            first = pl.multiple_of(index * tokens + part * count, count)
+            return ref.at[s, pl.ds(first, count)]
+
+        return Gather(ring, block, half, R.gs.at[slot], R.gr.at[slot])
+
+    h1_gather = [gather_rows(R.h1, s, s) for s in range(seqs)]
+    ct_gather = [gather_rows(R.ct, s, 2 + s) for s in range(seqs)]
+    h2_gather = [gather_rows(R.h2, s, 4 + s) for s in range(seqs)]
+    wo_gather = Gather(
+        ring,
+        lambda index: R.wo.at[:, index],
+        lambda index, part: R.wo.at[2 * part : 2 * part + 2, index],
+        R.gs.at[6],
+        R.gr.at[6],
+    )
+
+    for s in range(seqs):
+        lane = lax.broadcasted_iota(jnp.int32, (1, seq_len), 1)
+        half_rows = tokens // 2
+        pos = jnp.zeros((1, seq_len), jnp.int32)
+        down = lax.broadcasted_iota(jnp.int32, (half_rows, 128), 0)
+        for j in range(seq_len // half_rows):
+            start = R.order[s, j] * half_rows
+            pos = jnp.where(lane // half_rows == j, start, pos)
+            R.kpos[s, j * half_rows : (j + 1) * half_rows, :] = down + start
+        R.qpos[s] = pos + lane % half_rows
+
+    load_x.wait()
+
+    def params_row(row):
+        return jnp.concatenate([R.par[k, row : row + 1, :] for k in range(4)], axis=1)
+
+    def norm_one(s):
+        return row_norm(R.xb[s].astype(f32))
+
+    first = norm_one(0)
+    for copy in send_par:
+        copy.wait_recv()
+    gain1, shift1 = params_row(0), params_row(1)
+    R.h1[0, mine] = (first[0] * gain1 + shift1).astype(bf16)
+    h1_gather[0].start()
+    second = norm_one(1)
+    R.h1[1, mine] = (second[0] * gain1 + shift1).astype(bf16)
+    h1_gather[1].start()
+    load_o.wait()
+    send_o = to_planes(out_src, R.wo.at[layer, col], 4)
+    send_u = []
+    for g in range(4):
+        src = R.w_up.at[:, pl.ds(pl.multiple_of(g * width + col * hid, hid), hid)]
+        send_u += to_planes(src, R.wu.at[qkv_rows, g * hid : (g + 1) * hid], 5 + g)
+    send_d = to_planes(down_src, R.wd.at[down_rows], 9)
+
+    plane_lane = pl.ds(pl.multiple_of((col % 2) * head, head), head)
+    held = [R.par[k, :, plane_lane] for k in range(4)]
+
+    def held_row(first, parts):
+        total = jnp.zeros((1, head), f32)
+        for k, part in enumerate(parts):
+            total = jnp.where(col // 2 == k, part[first(k) : first(k) + 1, :], total)
+        return total
+
+    bias_q = held_row(lambda k: 2, held)
+    bias_v = held_row(lambda k: 3, held)
+    bias_u = jnp.concatenate(
+        [held_row(lambda k: 8 + k, [held[g]] * 4) for g in range(4)], axis=1
+    )
+    tile = 256
+
+    def project(s):
+        def body(t, _):
+            r = pl.ds(pl.multiple_of(t * tile, tile), tile)
+            both = dot_nn(R.h1[s, r, :], R.wq[...])
+            R.q[s, r, :] = (both[:, :head] + bias_q).astype(bf16)
+            R.k[s, r, :] = both[:, head : 2 * head].astype(bf16)
+            R.v[s, r, :] = (both[:, 2 * head :] + bias_v).astype(bf16)
+            return 0
+
+        lax.fori_loop(0, seq_len // tile, body, 0)
+        R.kt[s] = R.k[s].T
+        R.vt[s] = R.v[s].T
+
+    def masked(s, r, scores, other):
+        keys = jnp.concatenate([R.kpos[s]] * (tile // 128), axis=1)
+        return jnp.where(R.qpos[s, :, r] >= keys, scores, other)
+
+    def attend(s):
+        def body(t, _):
+            r = pl.ds(pl.multiple_of(t * tile, tile), tile)
+            raw = masked(s, r, dot_nt(R.k[s], R.q[s, r, :]), NEG_LARGE)
+            top = jnp.max(raw, axis=0, keepdims=True)
+            weights = jnp.exp2((raw - top) * step_c2)
+            total = jnp.sum(weights, axis=0, keepdims=True)
+            turned = dot_nn(R.vt[s], weights.astype(bf16)) * (1.0 / total)
+            R.ol[s, r, :] = turned.T.astype(bf16)
+            R.lse[s, :, r] = top * step_c2 + jnp.log2(total)
+            return 0
+
+        lax.fori_loop(0, seq_len // tile, body, 0)
+
+    others = (ring.dsib, ring.diag, ring.xsib, ring.xnb, ring.ysib, ring.ynb, ring.sib)
+
+    def heads_to_rows(s):
+        R.ob[s, :, pl.ds(head_cols, head)] = R.ol[s, mine, :]
+        copies = []
+        for slot, other in enumerate(others):
+            src = R.ol.at[s, pl.ds(pl.multiple_of(other * tokens, tokens), tokens)]
+            dst = R.ob.at[s, :, pl.ds(head_cols, head)]
+            copies.append(
+                send(src, dst, R.a_s.at[s, slot], R.a_r.at[s, slot], ring.flat(other))
+            )
+        return copies
+
+    def rows_to_heads(s):
+        R.dh[s, mine, :] = R.db[s, :, pl.ds(head_cols, head)]
+        copies = []
+        for slot, other in enumerate(others):
+            src = R.db.at[s, :, pl.ds(pl.multiple_of(other * head, head), head)]
+            dst = R.dh.at[s, mine]
+            copies.append(
+                send(src, dst, R.a_s.at[2 + s, slot], R.a_r.at[2 + s, slot], ring.flat(other))
+            )
+        return copies
+
+    h1_gather[0].relay()
+    h1_gather[0].relay_diag()
+    h1_gather[1].relay()
+    h1_gather[0].finish()
+    for copy in load_q:
+        copy.wait()
+    for copy in send_q:
+        copy.wait_recv()
+    project(0)
+    h1_gather[1].relay_diag()
+    for copy in send_o:
+        copy.wait_recv()
+    wo_gather.start()
+    for copy in load_ct:
+        copy.wait()
+    ct_gather[0].start()
+    attend(0)
+    moved_o = [heads_to_rows(0)]
+    wo_gather.relay()
+    ct_gather[0].relay()
+    h1_gather[1].finish()
+    project(1)
+    wo_gather.relay_diag()
+    ct_gather[0].relay_diag()
+    wo_gather.finish()
+    ct_gather[1].start()
+
+    bias_o = params_row(4)
+    gain2, shift2 = params_row(5), params_row(6)
+    out_w = R.wo
+
+    def out_project(s):
+        for copy in moved_o[s]:
+            copy.wait_recv()
+        weight = out_w[...].reshape(width, width)
+        resid = R.xb[s].astype(f32) + dot_nn(R.ob[s], weight) + bias_o
+        R.r1[s] = resid
+        normed, _ = row_norm(resid)
+        R.h2[s, mine] = (normed * gain2 + shift2).astype(bf16)
+
+    out_project(0)
+    h2_gather[0].start()
+    attend(1)
+    moved_o.append(heads_to_rows(1))
+    ct_gather[1].relay()
+    h2_gather[0].relay()
+    ct_gather[1].relay_diag()
+    h2_gather[0].relay_diag()
+    out_project(1)
+    h2_gather[1].start()
+    for copy in load_u:
+        copy.wait()
+    for copy in send_u:
+        copy.wait_recv()
+    load_d.wait()
+    for copy in send_d:
+        copy.wait_recv()
+    ct_gather[0].finish()
+    h2_gather[0].finish()
+
+    def feed(s):
+        def body(t, sums):
+            r = pl.ds(pl.multiple_of(t * tile, tile), tile)
+            hidden = dot_nn(R.h2[s, r, :], R.wu[...]) + bias_u
+            square = hidden * hidden
+            bend = jnp.tanh(hidden * (GELU_C + (GELU_C * GELU_K) * square))
+            half = 0.5 * (1.0 + bend)
+            active = (hidden * half).astype(bf16)
+            slope = half + (0.5 * hidden) * (1.0 - bend * bend) * (
+                GELU_C + (3.0 * GELU_C * GELU_K) * square
+            )
+            R.act[s, r, :] = active
+            R.po[s, r, :] = dot_nn(active, R.wd[...]).astype(bf16)
+            grad = dot_nt(R.ct[s, r, :], R.wd[...])
+            grad = (grad * slope).astype(bf16)
+            R.du[s, r, :] = grad
+            R.pd[s, r, :] = dot_nt(grad, R.wu[...]).astype(bf16)
+            return sums + jnp.sum(grad.astype(f32), axis=0, keepdims=True)
+
+        return lax.fori_loop(0, seq_len // tile, body, jnp.zeros((1, 4 * hid), f32))
+
+    def scatter(part, s, recv, slot, rows=None):
+        return Scatter(
+            ring,
+            part,
+            tokens,
+            R.r_sib.at[recv],
+            R.r_diag.at[recv],
+            R.r_side.at[recv],
+            R.ss.at[slot],
+            R.sr.at[slot],
+        )
+
+    up_sums = feed(0)
+    d2 = [scatter(R.pd.at[s], s, s, s) for s in range(2)]
+    out_sc = [scatter(R.po.at[s], s, 2 + s, 2 + s) for s in range(2)]
+    d2[0].start()
+    h2_gather[1].relay()
+    h2_gather[1].relay_diag()
+    d2[0].middle()
+    ct_gather[1].finish()
+    h2_gather[1].finish()
+    d2[0].last()
+    up_sums = up_sums + feed(1)
+    d2[1].start()
+
+    bz = R.bz
+    for g in range(4):
+        bz[2 + g : 3 + g, :] = up_sums[:, g * hid : (g + 1) * hid]
+
+    down_slots, up_slots = [], []
+
+    def grad_down():
+        for j in range(2):
+            cols = slice(j * 2 * hid, (j + 1) * 2 * hid)
+            total = dot_tn(R.act[0, :, cols], R.ct[0])
+            total = total + dot_tn(R.act[1, :, cols], R.ct[1])
+            R.gd[cols, :] = total.astype(bf16)
+
+    def grad_up():
+        for j in range(2):
+            cols = slice(j * 2 * hid, (j + 1) * 2 * hid)
+            total = dot_tn(R.du[0, :, cols], R.h2[0])
+            total = total + dot_tn(R.du[1, :, cols], R.h2[1])
+            total = total.T.astype(bf16).reshape(8, 4, 32, 2 * hid)
+            R.gu[:, :, :, cols] = total
+
+    def to_planes_part(piece, dst, slot):
+        return [
+            send(
+                piece(ring.up(hop)),
+                dst.at[hop - 1],
+                zs.at[slot, hop - 1],
+                zr.at[slot, hop - 1],
+                (col, ring.up(hop)),
+            )
+            for hop in range(1, 4)
+        ]
+
+    sums = {}
+
+    def back_norm2(s):
+        grad = d2[s].finish()
+        normed, inv_dev = row_norm(R.r1[s])
+        cot = R.ct[s, mine].astype(f32)
+        scaled = grad * gain2
+        resid = cot + inv_dev * (
+            scaled
+            - jnp.mean(scaled, axis=-1, keepdims=True)
+            - normed * jnp.mean(scaled * normed, axis=-1, keepdims=True)
+        )
+        R.dr[s] = resid
+        low = resid.astype(bf16)
+        R.dz[s] = low
+        lowf = low.astype(f32)
+        parts = (
+            jnp.sum(lowf, axis=0, keepdims=True),
+            jnp.sum(grad * normed, axis=0, keepdims=True),
+            jnp.sum(grad, axis=0, keepdims=True),
+            jnp.sum(cot, axis=0, keepdims=True),
+        )
+        for row, item in enumerate(parts):
+            sums[row] = sums[row] + item if row in sums else item
+        R.db[s] = dot_nt(low, out_w[...].reshape(width, width)).astype(bf16)
+
+    def attend_back(s):
+        R.dka[...] = jnp.zeros_like(R.dka)
+        R.dva[...] = jnp.zeros_like(R.dva)
+
+        def body(t, _):
+            r = pl.ds(pl.multiple_of(t * tile, tile), tile)
+            query, dout = R.q[s, r, :], R.dh[s, r, :]
+            raw = dot_nt(R.k[s], query)
+            probs = masked(s, r, jnp.exp2(raw * step_c2 - R.lse[s, :, r]), 0.0)
+            grad = dot_nt(R.v[s], dout)
+            R.dva[...] += dot_nn(probs.astype(bf16), dout)
+            delta = jnp.sum(probs * grad, axis=0, keepdims=True)
+            low = (probs * ((grad - delta) * scale)).astype(bf16)
+            R.dka[...] += dot_nn(low, query)
+            R.dp[s, r, :head] = dot_nn(R.kt[s], low).T.astype(bf16)
+            return 0
+
+        lax.fori_loop(0, seq_len // tile, body, 0)
+        R.dp[s, :, head : 2 * head] = R.dka[...].astype(bf16)
+        R.dp[s, :, 2 * head :] = R.dva[...].astype(bf16)
+
+    def first_part(s):
+        def body(t, _):
+            r = pl.ds(pl.multiple_of(t * tile, tile), tile)
+            R.pd[s, r, :] = dot_nt(R.dp[s, r, :], R.wq[...]).astype(bf16)
+            return 0
+
+        lax.fori_loop(0, seq_len // tile, body, 0)
+
+    back_norm2(0)
+    moved_d = [rows_to_heads(0)]
+    d2[1].middle()
+    grad_down()
+    z_down = to_planes_part(
+        lambda other: R.gd.at[pl.ds(pl.multiple_of(other * hid, hid), hid)], R.zd, 10
+    )
+    d2[1].last()
+    for copy in moved_d[0]:
+        copy.wait_recv()
+    attend_back(0)
+    back_norm2(1)
+    moved_d.append(rows_to_heads(1))
+    d2[0].drain()
+    first_part(0)
+    d1 = [scatter(R.pd.at[s], s, s, 4 + s) for s in range(2)]
+    d1[0].start()
+    grad_up()
+    z_up = to_planes_part(lambda other: R.gu.at[:, other], R.zu, 11)
+    d1[0].middle()
+    out_sc[0].start()
+    for copy in moved_d[1]:
+        copy.wait_recv()
+    d1[0].last()
+    out_sc[0].middle()
+    attend_back(1)
+    out_sc[0].last()
+    d2[1].drain()
+    first_part(1)
+    d1[1].start()
+    out_sc[1].start()
+
+    for g in range(3):
+        cols = slice(g * head, (g + 1) * head)
+        total = dot_tn(R.dp[0, :, cols], R.h1[0]) + dot_tn(R.dp[1, :, cols], R.h1[1])
+        R.gq[:, :, :, cols] = total.T.astype(bf16).reshape(8, 4, 32, head)
+    z_q = to_planes_part(lambda other: R.gq.at[:, other], R.zq, 12)
+    d1[1].middle()
+    out_sc[1].middle()
+    proj_sums = jnp.sum(R.dp[0].astype(f32), axis=0, keepdims=True) + jnp.sum(
+        R.dp[1].astype(f32), axis=0, keepdims=True
+    )
+    bz[0:1, :] = proj_sums[:, :head]
+    bz[1:2, :] = proj_sums[:, 2 * head :]
+    bz[6:8, :] = jnp.zeros((2, head), f32)
+    z_b = to_planes(bz, R.zb.at[layer], 13)
+    d1[1].last()
+    out_sc[1].last()
+
+    h2_flat = R.h2.at[0]
+    for copies in (h2_gather[0], h2_gather[1]):
+        copies.drain()
+    h2_flat[...] = (
+        dot_tn(R.ob[0], R.dz[0]) + dot_tn(R.ob[1], R.dz[1])
+    ).astype(bf16)
+    wo_sc = scatter(h2_flat, 0, 4, 6)
+    wo_sc.start()
+
+    owner_col, owner_layer = 2 * layer + col // 4, col % 4
+    at_home = owner_col * 4 + owner_layer == me
+    for copy in z_down:
+        copy.wait_recv()
+    total = R.gd[down_rows].astype(f32)
+    for k in range(3):
+        total = total + R.zd[k].astype(f32)
+    R.gdo[...] = total.astype(bf16)
+    wo_sc.middle()
+    for copy in z_b:
+        copy.wait_recv()
+    bz_all = bz[...] + (R.zb[ring.up(1)] + R.zb[ring.up(2)] + R.zb[ring.up(3)])
+    R.bzs[...] = bz_all
+    chosen = jnp.zeros((1, head), f32)
+    for k in range(4):
+        chosen = jnp.where(layer == k, bz_all[2 + k : 3 + k, :], chosen)
+    R.bu[...] = jnp.broadcast_to(chosen, (8, head))
+    psem = R.ps
+
+    @pl.when(at_home)
+    def _():
+        one = move(R.gdo, R.o_gd, psem.at[0])
+        two = move(R.bu, R.o_bu, psem.at[1])
+        one.wait()
+        two.wait()
+
+    def away():
+        where = (owner_col, owner_layer)
+        one = pltpu.make_async_remote_copy(
+            R.gdo, R.o_gd, psem.at[2], psem.at[3], where, pl.DeviceIdType.MESH
+        )
+        two = pltpu.make_async_remote_copy(
+            R.bu, R.o_bu, psem.at[4], psem.at[5], where, pl.DeviceIdType.MESH
+        )
+        return one, two
+
+    @pl.when(jnp.logical_not(at_home))
+    def _():
+        one, two = away()
+        one.start()
+        two.start()
+
+    for copy in z_up:
+        copy.wait_recv()
+    total = R.gu[:, layer].astype(f32)
+    for k in range(3):
+        total = total + R.zu[k].astype(f32)
+    R.guo[...] = total.astype(bf16)
+
+    def to_columns(src, dst, row):
+        keep = move(src.at[col], dst.at[col], local.at[12 + row])
+        copies = []
+        for slot, other in enumerate(others):
+            copies.append(
+                send(
+                    src.at[other],
+                    dst.at[col],
+                    R.a_s.at[4 + row, slot],
+                    R.a_r.at[4 + row, slot],
+                    ring.flat(other),
+                )
+            )
+        return keep, copies
+
+    up_keep, up_moves = to_columns(R.guo, R.o_gu, 0)
+    wo_sc.last()
+
+    bias_d = params_row(7)
+
+    def back_norm1(s):
+        grad = d1[s].finish()
+        normed, inv_dev = row_norm(R.xb[s].astype(f32))
+        scaled = grad * gain1
+        total = R.dr[s] + inv_dev * (
+            scaled
+            - jnp.mean(scaled, axis=-1, keepdims=True)
+            - normed * jnp.mean(scaled * normed, axis=-1, keepdims=True)
+        )
+        R.igs[s] = total.astype(bf16)
+        for row, item in ((4, grad * normed), (5, grad)):
+            item = jnp.sum(item, axis=0, keepdims=True)
+            sums[row] = sums[row] + item if row in sums else item
+
+    back_norm1(0)
+    back_norm1(1)
+    for row in range(6):
+        R.ev[row : row + 1, :] = sums[row]
+    R.ev[6:8, :] = jnp.zeros((2, width), f32)
+    save_ig = move(R.igs, R.o_ig, local.at[14])
+    ev_moves = []
+    for hop in range(1, 8):
+        other = (col + hop) % 8
+        ev_moves.append(
+            send(
+                R.ev.at[:, pl.ds(pl.multiple_of(other * head, head), head)],
+                R.evr.at[hop - 1],
+                R.es.at[hop - 1],
+                R.er.at[hop - 1],
+                ring.flat(other),
+            )
+        )
+    for copy in z_q:
+        copy.wait_recv()
+    total = R.gq[:, layer].astype(f32)
+    for k in range(3):
+        total = total + R.zq[k].astype(f32)
+    R.gqo[...] = total.astype(bf16)
+    q_keep, q_moves = to_columns(R.gqo, R.o_gq, 1)
+    for copy in ev_moves:
+        copy.wait_recv()
+    plane = R.ev[:, pl.ds(head_cols, head)]
+    for k in range(7):
+        plane = plane + R.evr[k]
+    R.evp[...] = plane
+    z_e = to_planes(R.evp, R.evz.at[layer], 14)
+    go_rows = pl.ds(pl.multiple_of(layer * 32, 32), 32)
+    own = wo_sc.finish()
+    R.gws[...] = own.astype(bf16)
+    z_o = to_planes_part(
+        lambda other: R.gws.at[pl.ds(pl.multiple_of(other * 32, 32), 32)], R.zo, 15
+    )
+    for s in range(2):
+        R.los[s] = (R.r1[s] + out_sc[s].finish() + bias_d).astype(bf16)
+    save_lo = move(R.los, R.o_lo, local.at[15])
+    for copy in z_e:
+        copy.wait_recv()
+    total = R.evp[...] + (R.evz[ring.up(1)] + R.evz[ring.up(2)] + R.evz[ring.up(3)])
+    both = jnp.concatenate([total, R.bzs[...]], axis=0)
+    picked = jnp.zeros((16, 32), f32)
+    for k in range(4):
+        picked = jnp.where(layer == k, both[:, k * 32 : (k + 1) * 32], picked)
+    R.o_small[...] = picked
+    for copy in z_o:
+        copy.wait_recv()
+    total = R.gws[go_rows].astype(f32)
+    for k in range(3):
+        total = total + R.zo[k].astype(f32)
+    R.o_go[...] = total
+
+    @pl.when(jnp.logical_not(at_home))
+    def _():
+        one, two = away()
+        one.wait()
+        two.wait()
+
+    save_ig.wait()
+    save_lo.wait()
+    for keep, copies in ((up_keep, up_moves), (q_keep, q_moves)):
+        keep.wait()
+        for copy in copies:
+            copy.wait()
+    for group in (h1_gather, ct_gather, [wo_gather], d1, out_sc, [wo_sc]):
+        for item in group:
+            item.drain()
+    for copies in (
+        moved_o + moved_d + [send_par, send_q, send_o, send_u, send_d]
+        + [z_down, z_up, z_q, z_b, z_e, z_o, ev_moves]
+    ):
+        for copy in copies:
+            copy.wait_send()
+
+def per_device_tp(
+    layer_in,
+    block_order,
+    ln1_gain,
+    ln1_shift,
+    w_qkv,
+    b_query,
+    b_value,
+    w_out,
+    b_out,
+    ln2_gain,
+    ln2_shift,
+    w_up,
+    b_up,
+    w_down,
+    b_down,
+    cotangent,
+):
+    f32, bf16, i32 = jnp.float32, jnp.bfloat16, jnp.int32
+    seqs, tokens, width = layer_in.shape
+    seq_len = tokens * 8
+    ff = w_up.shape[1]
+    hid = ff // 32
+    params = jnp.concatenate(
+        [
+            jnp.stack([ln1_gain, ln1_shift, b_query, b_value, b_out, ln2_gain, ln2_shift, b_down]),
+            b_up.reshape(4, -1),
+            jnp.zeros((4, width // 4), bf16),
+        ]
+    ).astype(f32)
+    anywhere = pl.BlockSpec(memory_space=pl.ANY)
+    in_vmem = pl.BlockSpec(memory_space=pltpu.VMEM)
+    inputs = dict(
+        order=(block_order, pl.BlockSpec(memory_space=pltpu.SMEM)),
+        params=(params, in_vmem),
+        x=(layer_in, anywhere),
+        cot=(cotangent, anywhere),
+        w_qkv=(w_qkv, anywhere),
+        w_out=(w_out, anywhere),
+        w_up=(w_up, anywhere),
+        w_down=(w_down, anywhere),
+    )
+    outputs = dict(
+        o_lo=((seqs, tokens, width), bf16, anywhere),
+        o_ig=((seqs, tokens, width), bf16, anywhere),
+        o_gq=((8, 32, 3 * HEAD_DIM), bf16, anywhere),
+        o_gu=((8, 32, 4 * hid), bf16, anywhere),
+        o_gd=((hid, width), bf16, anywhere),
+        o_go=((32, width), f32, in_vmem),
+        o_small=((16, 32), f32, in_vmem),
+        o_bu=((8, HEAD_DIM), f32, anywhere),
+    )
+    whole = (seqs, seq_len, width)
+    heads = (seqs, seq_len, HEAD_DIM)
+    turned = (seqs, HEAD_DIM, seq_len)
+    own = (seqs, tokens, width)
+    vmem, sems = pltpu.VMEM, pltpu.SemaphoreType.DMA
+    scratch = dict(
+        h1=vmem(whole, bf16),
+        ct=vmem(whole, bf16),
+        h2=vmem(whole, bf16),
+        po=vmem(whole, bf16),
+        pd=vmem(whole, bf16),
+        wq=vmem((width, 3 * HEAD_DIM), bf16),
+        wo=vmem((4, 8, 32, width), bf16),
+        wu=vmem((width, 4 * hid), bf16),
+        wd=vmem((4 * hid, width), bf16),
+        q=vmem(heads, bf16),
+        k=vmem(heads, bf16),
+        v=vmem(heads, bf16),
+        kt=vmem(turned, bf16),
+        vt=vmem(turned, bf16),
+        ol=vmem(heads, bf16),
+        dh=vmem(heads, bf16),
+        ob=vmem(own, bf16),
+        db=vmem(own, bf16),
+        xb=vmem(own, bf16),
+        dz=vmem(own, bf16),
+        igs=vmem(own, bf16),
+        los=vmem(own, bf16),
+        r1=vmem(own, f32),
+        dr=vmem(own, f32),
+        r_sib=vmem((5, 4, tokens, width), bf16),
+        r_diag=vmem((5, 2, tokens // 2, width), bf16),
+        r_side=vmem((5, 2, tokens, width), bf16),
+        kpos=vmem(heads, i32),
+        qpos=vmem((seqs, 1, seq_len), i32),
+        lse=vmem((seqs, 1, seq_len), f32),
+        act=vmem((seqs, seq_len, 4 * hid), bf16),
+        du=vmem((seqs, seq_len, 4 * hid), bf16),
+        dp=vmem((seqs, seq_len, 3 * HEAD_DIM), bf16),
+        dka=vmem((seq_len, HEAD_DIM), f32),
+        dva=vmem((seq_len, HEAD_DIM), f32),
+        gd=vmem((4 * hid, width), bf16),
+        gu=vmem((8, 4, 32, 4 * hid), bf16),
+        gq=vmem((8, 4, 32, 3 * HEAD_DIM), bf16),
+        gws=vmem((tokens, width), bf16),
+        gdo=vmem((hid, width), bf16),
+        guo=vmem((8, 32, 4 * hid), bf16),
+        gqo=vmem((8, 32, 3 * HEAD_DIM), bf16),
+        zd=vmem((3, hid, width), bf16),
+        zu=vmem((3, 8, 32, 4 * hid), bf16),
+        zq=vmem((3, 8, 32, 3 * HEAD_DIM), bf16),
+        zo=vmem((3, 32, width), bf16),
+        par=vmem((4, SMALL_ROWS, width // 4), f32),
+        bz=vmem((8, HEAD_DIM), f32),
+        bzs=vmem((8, HEAD_DIM), f32),
+        bu=vmem((8, HEAD_DIM), f32),
+        zb=vmem((4, 8, HEAD_DIM), f32),
+        ev=vmem((8, width), f32),
+        evr=vmem((7, 8, HEAD_DIM), f32),
+        evp=vmem((8, HEAD_DIM), f32),
+        evz=vmem((4, 8, HEAD_DIM), f32),
+        lsem=sems((16,)),
+        zs=sems((16, 3)),
+        zr=sems((16, 3)),
+        gs=sems((7, 8)),
+        gr=sems((7, 8)),
+        ss=sems((7, 8)),
+        sr=sems((7, 8)),
+        a_s=sems((6, 7)),
+        a_r=sems((6, 7)),
+        es=sems((7,)),
+        er=sems((7,)),
+        ps=sems((6,)),
+    )
+    names = list(inputs) + list(outputs) + list(scratch)
+
+    def body(*refs):
+        layer_kernel(HEAD_DIM ** (-0.5), types.SimpleNamespace(**dict(zip(names, refs))))
+
+    results = pl.pallas_call(
+        body,
+        out_shape=[jax.ShapeDtypeStruct(shape, kind) for shape, kind, _ in outputs.values()],
+        in_specs=[spec for _, spec in inputs.values()],
+        out_specs=[spec for _, _, spec in outputs.values()],
+        scratch_shapes=list(scratch.values()),
+        compiler_params=pltpu.CompilerParams(
+            collective_id=0, has_side_effects=True, vmem_limit_bytes=VMEM_BYTES
+        ),
+    )(*(item for item, _ in inputs.values()))
+    got = types.SimpleNamespace(**dict(zip(outputs, results)))
+
+    def by_columns(item, groups):
+        item = item.reshape(8, 32, groups, -1).astype(f32)
+        return jnp.transpose(item, (1, 2, 0, 3)).reshape(32, -1)
+
+    small = got.o_small
+    return (
+        got.o_lo,
+        got.o_ig,
+        small[4],
+        small[5],
+        by_columns(got.o_gq, 3),
+        small[8],
+        small[9],
+        got.o_go,
+        small[0],
+        small[1],
+        small[2],
+        by_columns(got.o_gu, 4),
+        got.o_bu[0],
+        got.o_gd.astype(f32),
+        small[3],
+    )
+
+
 def solution(mesh):
     placed = (
         P("fsdp", "ctx", None),
@@ -341,8 +1296,9 @@
         P("fsdp"),
         P("fsdp", "ctx", None),
     )
+    by_heads = mesh.shape["ctx"] == HEADS and mesh.shape["fsdp"] == 4
     return jax.shard_map(
-        per_device,
+        per_device_tp if by_heads else per_device_ctx,
         mesh=mesh,
         in_specs=placed,
         out_specs=(

time: 1860 us -> 233 us (0.13)
  waiting for transfers between devices: 1460 us -> 0 us
  Pallas kernels: 0 us -> 216 us
  matrix products: 130 us -> 0 us
  blocking collectives: 125 us -> 0 us
  local copies, waits for them, and re-layouts: 97.7 us -> 14.6 us
  other arithmetic: 28.4 us -> 1.45 us
    reduce_scatter x6 -> x0, waiting for transfers between devices: 1020 us -> none  [the longest x1 366 us: per_device(): lax.psum_scatter(totals[11], ('ctx', 'fsdp'), scatter_dimension=0, tiled=...]
    all_gather x8 -> x0, waiting for transfers between devices: 437 us -> none  [the longest x1 146 us: per_device(): lax.all_gather(w_up, 'fsdp', axis=0, tiled=True)]
    pallas_call x0 -> x1, Pallas kernels: none -> 216 us  [per_device_tp(): pl.pallas_call(body, out_shape=[jax.ShapeDtypeStruct(shape, kind) for sha...]
    dot_general x60 -> x0, matrix products: 130 us -> none  [the longest x8 16.4 us: block_probs(): jnp.einsum('qhd,khd->hqk', query_heads, key_heads, preferred_element_type...]
    all_gather x9 -> x0, blocking collectives: 86.2 us -> none  [the longest x1 12.6 us: per_device(): lax.all_gather(ln1_shift, 'fsdp', axis=0, tiled=True)]
    dynamic_update_slice x8 -> x0, local copies, waits for them, and re-layouts: 41 us -> none  [per_device(): lax.scan(backward_step, jnp.zeros((tokens, HEADS, HEAD_DIM), jnp.float32)...]
    unnamed x1 -> x0, blocking collectives: 38.9 us -> none
    unnamed x203 -> x15, local copies, waits for them, and re-layouts: 33.6 us -> 4.18 us
  transfers between devices with their start and end apart: 14 -> 0, of which waited for: 12 -> 0; matrix products, arithmetic and copies ran while one was open for 9% -> 0% of each run, Pallas kernels for 0% -> 0%
where the time goes in v2:
time: 233 us
  Pallas kernels  216 us (93%)
  local copies, waits for them, and re-layouts  14.6 us (6%)
    pallas_call x1, Pallas kernels, per_device_tp(): pl.pallas_call(body, out_shape=[jax.ShapeDtypeStruct(shape, kind) for sha...  216 us
    another operation x8, local copies, waits for them, and re-layouts, per_device_tp(): jnp.stack([ln1_gain, ln1_shift, b_query, b_value, b_out, ln2_gain, ln2_sh...  5.26 us

profile of v2, /device:TPU:0, one launch (start us, length us, event | category | flops | bytes accessed | tf_op | source)
XLA Modules:
  0.0 232.6 jit_solution(9423537567495763590)
XLA Ops:
  0.6 0.7 stack.24
  1.3 0.7 stack.25
  2.0 0.7 stack.26
  2.6 0.7 stack.27
  3.3 0.7 stack.28
  3.9 0.7 stack.29
  4.6 0.7 stack.30
  5.3 0.7 stack.31
  5.9 0.7 reshape.51
  6.6 0.1 concatenate.3
  6.7 0.6 convert_element_type.14.refs_1_
  7.3 215.8 %shard_map.271 = (bf16[2,128,1024]{2,1,0:T(8,128)(2,1)}, bf16[2,128,1024]{2,1,0:T(8,128)(2,1)}, bf16[8,32,384]{2,1,0:T(8,128)(2,1)}, bf16[8,32,512]{2,1,0:T(8,12...) custom-call(s32[2,16]{1,0:T(2,128)} %refs_0_.1, ...), custom_call_target="tpu_custom_call" | custom-call | tf_op jit(solution)/shard_map/pallas_call | solution.py:1244
  223.1 0.0 copy-start.3
  223.1 1.2 slice_bitcast_fusion.1
  224.3 1.4 slice_bitcast_fusion
  225.8 1.1 reshape.63
  226.8 0.0 copy-start.2
  226.8 0.2 copy.34
  227.1 0.0 copy-start.1
  227.1 0.8 copy.41
  227.9 0.0 copy-done.3
  227.9 0.2 reshape.65
  228.1 0.0 copy-start
  228.1 0.3 copy.35
  228.4 0.0 copy-start.4
  228.4 1.1 copy.40
  229.5 0.0 copy-done.2
  229.5 0.8 convert_element_type.17
  230.4 0.0 copy-done.1
  230.4 0.8 copy.45
  231.2 0.0 copy-done
  231.2 0.8 copy.46
  232.0 0.0 copy-done.4
  232.0 0.7 copy.47
  (1 shorter events, 0.0 us)
Async XLA Ops:
  223.1 4.8 %copy-start.3 = (bf16[8,32,512]{2,1,0:T(8,128)(2,1)S(1)}, bf16[8,32,512]{2,1,0:T(8,128)(2,1)}, u32[]{:S(2)}) copy-start(bf16[8,32,512]{2,1,0:T(8,128)(2,1)} %get-tuple-element.28) | copy-start | bytes 786436
  226.8 2.7 %copy-start.2 = (bf16[128,1024]{1,0:T(8,128)(2,1)S(1)}, bf16[128,1024]{1,0:T(8,128)(2,1)}, u32[]{:S(2)}) copy-start(bf16[128,1024]{1,0:T(8,128)(2,1)} %get-tuple-element.30) | copy-start | bytes 786436
  227.1 3.3 %copy-start.1 = (bf16[2,128,1024]{2,1,0:T(8,128)(2,1)S(1)}, bf16[2,128,1024]{2,1,0:T(8,128)(2,1)}, u32[]{:S(2)}) copy-start(bf16[2,128,1024]{2,1,0:T(8,128)(2,1)} %get-tuple-element.54) | copy-start | bytes 1572868
  228.1 3.1 %copy-start = (bf16[2,128,1024]{2,1,0:T(8,128)(2,1)S(1)}, bf16[2,128,1024]{2,1,0:T(8,128)(2,1)}, u32[]{:S(2)}) copy-start(bf16[2,128,1024]{2,1,0:T(8,128)(2,1)} %get-tuple-element.55) | copy-start | bytes 1572868
  228.4 3.6 %copy-start.4 = (f32[32,1024]{1,0:T(8,128)S(1)}, f32[32,1024]{1,0:T(8,128)}, u32[]{:S(2)}) copy-start(f32[32,1024]{1,0:T(8,128)} %get-tuple-element.61) | copy-start | bytes 393220
